TPU v7x, 32 devices: a whole 2x2x4 slice. The times are simulated.
32 devices in a mesh: ctx: 16 (over z, y, core), tp: 2 (over x).
Axes of the slice: x: 2, y: 2, z: 4, core: 2. Of those that a mesh axis runs over, the one named last changes fastest.
Arguments:
- query: bfloat16 [4096, 8192], P('ctx', 'tp'), may hold values from -20 to 20
- key: bfloat16 [4096, 1024], P('ctx', 'tp'), may hold values from -4 to 4
- value: bfloat16 [4096, 1024], P('ctx', 'tp'), may hold values from -6 to 6
- output_cotangent: bfloat16 [4096, 8192], P('ctx', 'tp'), may hold values from -6 to 6
- parents: int32 [32], replicated, may hold values from 0 to 30, as said below
Outputs:
- attn_out: bfloat16 [4096, 8192], P('ctx', 'tp')
- grad_query: bfloat16 [4096, 8192], P('ctx', 'tp')
- grad_key: bfloat16 [4096, 1024], P('ctx', 'tp')
- grad_value: bfloat16 [4096, 1024], P('ctx', 'tp')
Inputs may be any that keep to these rules, and one draw needn't show every extreme that they name: parents[0] = 0 and parents[b] < b for every other block b; every ancestor of a block, other than block 0, lies on the block's own index of ctx or on one of the 3 indices before it. In every draw, the blocks of index 3 of ctx, and of every index of ctx that is a positive multiple of 4, read ancestors held by each of the 3 indices before it.
All inputs are finite; a program needn't handle non-finite values.
Results may differ from a plain program's by a relative error of at most 0.0091.
Values may be sent and summed in bfloat16 or wider, within the bound.
No kernel may reach another device: no remote copies, remote signals or barrier semaphores. Data moves between devices by JAX's collectives and lax.ppermute only.
A program may use at most 128 MiB of HBM per device.

v0:
```python
import functools
import math

import jax
import jax.numpy as jnp
from jax import lax
from jax.experimental import pallas as pl
from jax.experimental.pallas import tpu as pltpu
from jax.sharding import PartitionSpec as P

HEAD_WIDTH = 128
BLOCK_TOKENS = 128
HOPS = 3
CHUNK_HEADS = 4


def passed_along(array, by):
    devices = lax.axis_size("ctx")
    pairs = [(i, i + by) for i in range(devices) if 0 <= i + by < devices]
    return lax.ppermute(array, "ctx", pairs)


def tree_stages(devices):
    stages = []
    size = devices
    while size > 1:
        fan = 4 if size % 4 == 0 else (2 if size % 2 == 0 else size)
        size //= fan
        stages.append((size, fan))
    return stages


def spread_from_first(value):
    devices = lax.axis_size("ctx")
    held = jnp.where(lax.axis_index("ctx") == 0, value, 0).astype(value.dtype)
    for stride, fan in tree_stages(devices):
        arrived = [
            lax.ppermute(
                held, "ctx", [(i, i + j * stride) for i in range(0, devices, stride * fan)]
            )
            for j in range(1, fan)
        ]
        for piece in arrived:
            held = held + piece
    return held


def sum_to_first(terms):
    devices = lax.axis_size("ctx")
    total = terms.astype(jnp.float32)
    for stride, fan in reversed(tree_stages(devices)):
        sent = total.astype(jnp.bfloat16)
        for j in range(1, fan):
            total = total + lax.ppermute(
                sent, "ctx", [(i + j * stride, i) for i in range(0, devices, stride * fan)]
            ).astype(jnp.float32)
    return total


def export_kernel(blocks_here, parents_ref, choice_ref, reach_ref):
    block_count = parents_ref.shape[0]
    devices = block_count // blocks_here

    @pl.loop(0, block_count)
    def _(b):
        reach_ref[b] = b // blocks_here

    @pl.loop(0, block_count)
    def _(step):
        b = block_count - 1 - step
        up = parents_ref[b]
        reach_ref[up] = jnp.maximum(reach_ref[up], reach_ref[b])

    def visit(device, crowded):
        count = jnp.int32(0)
        choice = jnp.int32(0)
        for slot in range(blocks_here):
            block = device * blocks_here + slot
            read = ((reach_ref[block] > device) & (block > 0)).astype(jnp.int32)
            count = count + read
            choice = jnp.where(read > 0, slot, choice)
        choice_ref[device] = choice
        return jnp.maximum(crowded, count)

    choice_ref[devices] = lax.fori_loop(0, devices, visit, jnp.int32(0))


def exported_blocks(parents, blocks_here):
    block_count = parents.shape[0]
    return pl.pallas_call(
        functools.partial(export_kernel, blocks_here),
        out_shape=jax.ShapeDtypeStruct((block_count // blocks_here + 1,), jnp.int32),
        in_specs=[pl.BlockSpec(memory_space=pltpu.SMEM)],
        out_specs=pl.BlockSpec(memory_space=pltpu.SMEM),
        scratch_shapes=[pltpu.SMEM((block_count,), jnp.int32)],
        name="exported",
    )(parents)


NT = (((1,), (1,)), ((), ()))
NN = (((1,), (0,)), ((), ()))
TN = (((0,), (0,)), ((), ()))


def dot(a, b, dims):
    return lax.dot_general(a, b, dims, preferred_element_type=jnp.float32)


def attention_kernel(
    carried, blocks_here, heads_per_group, parents_ref, q_ref, do_ref, k_own, v_own, root_ref,
    *rest,
):
    pieces = rest[:HOPS]
    (out_ref, gq_ref, gown_ref, groot_ref) = rest[HOPS : HOPS + 4]
    gpieces = rest[HOPS + 4 : 2 * HOPS + 4]
    k_all, v_all, gk_acc, gv_acc, slots, counts = rest[2 * HOPS + 4 :]
    own_base = 1 + HOPS * carried
    slot_count = own_base + blocks_here
    scale = 1.0 / math.sqrt(HEAD_WIDTH)
    log2e = math.log2(math.e)
    rows = CHUNK_HEADS * BLOCK_TOKENS

    @pl.when(pl.program_id(0) == 0)
    def _():
        position = lax.axis_index("ctx")
        for qb in range(blocks_here):
            own = position * blocks_here + qb
            slots[qb, 0] = 0

            def climb(step, state):
                current, count = state
                current = parents_ref[current]
                device = lax.div(current, blocks_here)
                slot = lax.rem(current, blocks_here)
                back = position - device
                far = 1 + (HOPS - back) * carried + (slot if carried > 1 else 0)
                where_held = jnp.where(back == 0, own_base + slot, far)
                seen = (current > 0) & (back <= HOPS)

                @pl.when(seen)
                def _():
                    slots[qb, count] = where_held

                return current, count + seen.astype(jnp.int32)

            _, count = lax.fori_loop(
                0, (HOPS + 1) * blocks_here, climb, (own, jnp.int32(1))
            )

            @pl.when(own > 0)
            def _():
                slots[qb, count] = own_base + qb

            counts[qb] = jnp.where(own > 0, count + 1, 1)

    k_all[0] = root_ref[0]
    v_all[0] = root_ref[1]
    for at, piece in enumerate(pieces):
        for e in range(carried):
            k_all[1 + at * carried + e] = piece[0, e * BLOCK_TOKENS : (e + 1) * BLOCK_TOKENS]
            v_all[1 + at * carried + e] = piece[1, e * BLOCK_TOKENS : (e + 1) * BLOCK_TOKENS]
    for b in range(blocks_here):
        k_all[own_base + b] = k_own[b * BLOCK_TOKENS : (b + 1) * BLOCK_TOKENS]
        v_all[own_base + b] = v_own[b * BLOCK_TOKENS : (b + 1) * BLOCK_TOKENS]
    gk_acc[...] = jnp.zeros_like(gk_acc)
    gv_acc[...] = jnp.zeros_like(gv_acc)

    def run_block(qb, seen):
        held = [slots[qb, j] for j in range(seen)]
        tokens = pl.ds(pl.multiple_of(qb * BLOCK_TOKENS, BLOCK_TOKENS), BLOCK_TOKENS)

        def run_chunk(chunk, carry):
            cols = [
                pl.ds(pl.multiple_of((chunk * CHUNK_HEADS + h) * HEAD_WIDTH, HEAD_WIDTH), HEAD_WIDTH)
                for h in range(CHUNK_HEADS)
            ]
            q = jnp.concatenate([q_ref[tokens, c] for c in cols], axis=0)
            do = jnp.concatenate([do_ref[tokens, c] for c in cols], axis=0)
            keys = [k_all[s] for s in held]
            values = [v_all[s] for s in held]
            scores = [dot(q, k, NT) for k in keys]
            token = lax.broadcasted_iota(jnp.int32, (rows, BLOCK_TOKENS), 0) % BLOCK_TOKENS
            other = lax.broadcasted_iota(jnp.int32, (rows, BLOCK_TOKENS), 1)
            scores[-1] = jnp.where(other <= token, scores[-1], -jnp.inf)
            top = functools.reduce(jnp.maximum, scores)
            top = jnp.max(top, axis=1, keepdims=True) * (scale * log2e)
            raised = [jnp.exp2(s * (scale * log2e) - top) for s in scores]
            total = jnp.sum(functools.reduce(jnp.add, raised), axis=1, keepdims=True)
            inverse = 1.0 / total
            probs = [r * inverse for r in raised]
            weights = [p.astype(jnp.bfloat16) for p in probs]
            attended = functools.reduce(
                jnp.add, [dot(w, v, NN) for w, v in zip(weights, values)]
            ).astype(jnp.bfloat16)
            delta = jnp.sum(
                do.astype(jnp.float32) * attended.astype(jnp.float32), axis=1, keepdims=True
            )
            dscores = [
                (p * (dot(do, v, NT) - delta)).astype(jnp.bfloat16) for p, v in zip(probs, values)
            ]
            grad_q = functools.reduce(
                jnp.add, [dot(d, k, NN) for d, k in zip(dscores, keys)]
            )
            grad_q = (grad_q * scale).astype(jnp.bfloat16)
            for h, c in enumerate(cols):
                part = slice(h * BLOCK_TOKENS, (h + 1) * BLOCK_TOKENS)
                out_ref[tokens, c] = attended[part]
                gq_ref[tokens, c] = grad_q[part]
            for s, d, w in zip(held, dscores, weights):
                gk_acc[s] += dot(q, d, TN)
                gv_acc[s] += dot(do, w, TN)
            return carry

        lax.fori_loop(0, heads_per_group // CHUNK_HEADS, run_chunk, 0)

    @pl.loop(0, blocks_here)
    def _(qb):
        seen_here = counts[qb]
        for seen in range(1, slot_count + 1):
            pl.when(seen_here == seen)(functools.partial(run_block, qb, seen))

    def grads(slot):
        return (gk_acc[slot] * scale).T, gv_acc[slot].T

    for b in range(blocks_here):
        part = slice(b * BLOCK_TOKENS, (b + 1) * BLOCK_TOKENS)
        gown_ref[0, part], gown_ref[1, part] = grads(own_base + b)
    groot_ref[0], groot_ref[1] = grads(0)
    for at, piece in enumerate(gpieces):
        for e in range(carried):
            part = slice(e * BLOCK_TOKENS, (e + 1) * BLOCK_TOKENS)
            gk, gv = grads(1 + at * carried + e)
            piece[0, part] = gk.astype(jnp.bfloat16)
            piece[1, part] = gv.astype(jnp.bfloat16)


def attention(carried, parents, query, grad, key, value, root_pair, pieces):
    tokens_here = query.shape[0]
    blocks_here = tokens_here // BLOCK_TOKENS
    groups = key.shape[1] // HEAD_WIDTH
    heads_per_group = query.shape[1] // HEAD_WIDTH // groups
    wide = pl.BlockSpec((tokens_here, heads_per_group * HEAD_WIDTH), lambda g, _: (0, g))
    narrow = pl.BlockSpec((tokens_here, HEAD_WIDTH), lambda g, _: (0, g))
    pair = lambda count: pl.BlockSpec((2, count, HEAD_WIDTH), lambda g, _: (0, 0, g))
    root_spec = pair(BLOCK_TOKENS)
    piece_spec = pair(carried * BLOCK_TOKENS)
    own_spec = pair(tokens_here)
    slot_count = 1 + HOPS * carried + blocks_here
    pair_shape = lambda like, kind: jax.ShapeDtypeStruct(like.shape, kind)
    blocks = pltpu.VMEM((slot_count, BLOCK_TOKENS, HEAD_WIDTH), jnp.bfloat16)
    sums = pltpu.VMEM((slot_count, HEAD_WIDTH, BLOCK_TOKENS), jnp.float32)
    return pl.pallas_call(
        functools.partial(attention_kernel, carried, blocks_here, heads_per_group),
        grid_spec=pltpu.PrefetchScalarGridSpec(
            num_scalar_prefetch=1,
            grid=(groups,),
            in_specs=[wide, wide, narrow, narrow, root_spec] + [piece_spec] * HOPS,
            out_specs=[wide, wide, own_spec, root_spec] + [piece_spec] * HOPS,
            scratch_shapes=[
                blocks,
                blocks,
                sums,
                sums,
                pltpu.SMEM((blocks_here, slot_count), jnp.int32),
                pltpu.SMEM((blocks_here,), jnp.int32),
            ],
        ),
        out_shape=[
            pair_shape(query, jnp.bfloat16),
            pair_shape(query, jnp.bfloat16),
            jax.ShapeDtypeStruct((2,) + key.shape, jnp.float32),
            pair_shape(root_pair, jnp.float32),
        ]
        + [pair_shape(p, jnp.bfloat16) for p in pieces],
        compiler_params=pltpu.CompilerParams(vmem_limit_bytes=48 << 20),
        name=f"tree_attention_{carried}",
    )(parents, query, grad, key, value, root_pair, *pieces)


def run(carried, choice, query, key, value, output_cotangent, parents):
    tokens_here = query.shape[0]
    blocks_here = tokens_here // BLOCK_TOKENS
    position = lax.axis_index("ctx")
    key_value = jnp.stack([key, value])
    root_pair = spread_from_first(key_value[:, :BLOCK_TOKENS])
    if carried == blocks_here:
        sent = key_value
    else:
        mine = choice[position]
        sent = lax.dynamic_slice_in_dim(key_value, mine * BLOCK_TOKENS, BLOCK_TOKENS, 1)
    pieces = [passed_along(sent, back) for back in range(HOPS, 0, -1)]
    out, grad_q, own, root_terms, *terms = attention(
        carried, parents, query, output_cotangent, key, value, root_pair, pieces
    )
    returned = sum(
        passed_along(terms[HOPS - back], -back).astype(jnp.float32)
        for back in range(1, HOPS + 1)
    )
    root_sum = sum_to_first(root_terms)
    root_rows = jnp.where(position == 0, root_sum, 0.0)
    parts = []
    for b in range(blocks_here):
        rows = slice(b * BLOCK_TOKENS, (b + 1) * BLOCK_TOKENS)
        part = own[:, rows]
        if carried == blocks_here:
            part = part + returned[:, rows]
        else:
            part = part + jnp.where(mine == b, returned, 0.0)
        if b == 0:
            part = part + root_rows
        parts.append(part)
    total = jnp.concatenate(parts, axis=1).astype(jnp.bfloat16)
    return out, grad_q, total[0], total[1]


def local(query, key, value, output_cotangent, parents):
    blocks_here = query.shape[0] // BLOCK_TOKENS
    choice = exported_blocks(parents, blocks_here)
    operands = (choice, query, key, value, output_cotangent, parents)
    return lax.cond(
        choice[-1] > 1,
        functools.partial(run, blocks_here),
        functools.partial(run, 1),
        *operands,
    )


def solution(mesh):
    in_specs = (P("ctx", "tp"), P("ctx", "tp"), P("ctx", "tp"), P("ctx", "tp"), P())
    out_specs = (P("ctx", "tp"), P("ctx", "tp"), P("ctx", "tp"), P("ctx", "tp"))
    return jax.shard_map(local, mesh=mesh, in_specs=in_specs, out_specs=out_specs, check_vma=False)
```

profile of v0, /device:TPU:0, one launch (start us, length us, event | category | flops | bytes accessed | tf_op | source)
XLA Modules:
  0.0 109.0 jit_solution(2356641404705503192)
XLA Ops:
  0.6 2.0 %exported.1 = s32[17]{0:T(128)S(1)} custom-call(s32[32]{0:T(128)} %parents_ref.1), custom_call_target="tpu_custom_call" | custom-call | tf_op jit(solution)/shard_map/exported/pallas_call | solution.py:90
  3.9 105.1 %conditional.1 = (bf16[256,4096]{1,0:T(8,128)(2,1)}, bf16[256,4096]{1,0:T(8,128)(2,1)}, bf16[256,512]{1,0:T(8,128)(2,1)}, bf16[256,512]{1,0:T(8,128)(2,1)}) conditional(s32[]{:T(128)} %bitcast.11, (bf16[256,512]{1,0:T(8,128)(2,1)}, bf16[256,512]{1,0:T(8,128)(2,1)}, s32[17]{0:T(128)S(1)}, s32[32]{0:T(128)}, bf16[256,4096]{1,0:T(8,128)(2,1)}, ...), branch_computations={%region_0.1_spmd, %region_1.2_spmd} | conditional | flops 7340045 | bytes 59508132 | solution.py:320
  4.0 0.6 dynamic_slice.4
  5.4 1.1 %fusion.2 = (bf16[2,128,512]{2,1,0:T(8,128)(2,1)S(1)}, bf16[2,128,512]{2,1,0:T(8,128)(2,1)S(1)}) fusion(s32[]{:T(128)S(6)} %select_n.33, bf16[1,256,512]{2,1,0:T(8,128)(2,1)} %bitcast.16, bf16[1,256,512]{2,1,0:T(8,128)(2,1)} %bitcast.20, pred[]{:T(512)S(6)} %eq.14), kind=kLoop, calls=%fused_computation.12 | loop fusion | flops 1179648 | bytes 1048581 | tf_op jit(solution)/shard_map/cond/branch_0_fun/stack | solution.py:284
  6.5 7.0 %collective-permute-start.2 = (bf16[2,128,512]{2,1,0:T(8,128)(2,1)S(1)}, bf16[2,128,512]{2,1,0:T(8,128)(2,1)S(1)}, u32[]{:S(2)}, u32[]{:S(2)}) collective-permute-start(bf16[2,128,512]{2,1,0:T(8,128)(2,1)S(1)} %get-tuple-element.58), channel_id=1, source_target_pairs={{0,24},{1,25}} | collective-permute-start | bytes 786440 | tf_op jit(solution)/shard_map/cond/branch_0_fun/ppermute | solution.py:38
  13.5 1.3 %collective-permute-start.1 = (bf16[2,128,512]{2,1,0:T(8,128)(2,1)S(1)}, bf16[2,128,512]{2,1,0:T(8,128)(2,1)S(1)}, u32[]{:S(2)}, u32[]{:S(2)}) collective-permute-start(bf16[2,128,512]{2,1,0:T(8,128)(2,1)S(1)} %get-tuple-element.58), channel_id=1, source_target_pairs={{0,16},{1,17}} | collective-permute-start | bytes 786440 | tf_op jit(solution)/shard_map/cond/branch_0_fun/ppermute | solution.py:38
  14.8 1.3 %collective-permute-start = (bf16[2,128,512]{2,1,0:T(8,128)(2,1)S(1)}, bf16[2,128,512]{2,1,0:T(8,128)(2,1)S(1)}, u32[]{:S(2)}, u32[]{:S(2)}) collective-permute-start(bf16[2,128,512]{2,1,0:T(8,128)(2,1)S(1)} %get-tuple-element.58), channel_id=1, source_target_pairs={{0,8},{1,9}} | collective-permute-start | bytes 786440 | tf_op jit(solution)/shard_map/cond/branch_0_fun/ppermute | solution.py:38
  16.1 1.2 %collective-permute-done.2 = bf16[2,128,512]{2,1,0:T(8,128)(2,1)S(1)} collective-permute-done((bf16[2,128,512]{2,1,0:T(8,128)(2,1)S(1)}, bf16[2,128,512]{2,1,0:T(8,128)(2,1)S(1)}, u32[]{:S(2)}, u32[]{:S(2)}) %collective-permute-start.2) | collective-permute-done | bytes 262176 | tf_op jit(solution)/shard_map/cond/branch_0_fun/ppermute | solution.py:38
  17.4 2.8 %collective-permute-done.1 = bf16[2,128,512]{2,1,0:T(8,128)(2,1)S(1)} collective-permute-done((bf16[2,128,512]{2,1,0:T(8,128)(2,1)S(1)}, bf16[2,128,512]{2,1,0:T(8,128)(2,1)S(1)}, u32[]{:S(2)}, u32[]{:S(2)}) %collective-permute-start.1) | collective-permute-done | bytes 262176 | tf_op jit(solution)/shard_map/cond/branch_0_fun/ppermute | solution.py:38
  20.2 2.8 %collective-permute-done = bf16[2,128,512]{2,1,0:T(8,128)(2,1)S(1)} collective-permute-done((bf16[2,128,512]{2,1,0:T(8,128)(2,1)S(1)}, bf16[2,128,512]{2,1,0:T(8,128)(2,1)S(1)}, u32[]{:S(2)}, u32[]{:S(2)}) %collective-permute-start) | collective-permute-done | bytes 262176 | tf_op jit(solution)/shard_map/cond/branch_0_fun/ppermute | solution.py:38
  23.0 1.3 %collective-permute-start.5 = (bf16[2,128,512]{2,1,0:T(8,128)(2,1)S(1)}, bf16[2,128,512]{2,1,0:T(8,128)(2,1)S(1)}, u32[]{:S(2)}, u32[]{:S(2)}) collective-permute-start(bf16[2,128,512]{2,1,0:T(8,128)(2,1)S(1)} %add_add_fusion.1), channel_id=1, source_target_pairs={{0,6},{8,14},{16,22},{24,30},{1,7},{9,15},{17,23},{25,31}} | collective-permute-start | bytes 786440 | tf_op jit(solution)/shard_map/cond/branch_0_fun/ppermute | solution.py:38
  24.3 1.3 %collective-permute-start.4 = (bf16[2,128,512]{2,1,0:T(8,128)(2,1)S(1)}, bf16[2,128,512]{2,1,0:T(8,128)(2,1)S(1)}, u32[]{:S(2)}, u32[]{:S(2)}) collective-permute-start(bf16[2,128,512]{2,1,0:T(8,128)(2,1)S(1)} %add_add_fusion.1), channel_id=1, source_target_pairs={{0,4},{8,12},{16,20},{24,28},{1,5},{9,13},{17,21},{25,29}} | collective-permute-start | bytes 786440 | tf_op jit(solution)/shard_map/cond/branch_0_fun/ppermute | solution.py:38
  25.7 1.3 %collective-permute-start.3 = (bf16[2,128,512]{2,1,0:T(8,128)(2,1)S(1)}, bf16[2,128,512]{2,1,0:T(8,128)(2,1)S(1)}, u32[]{:S(2)}, u32[]{:S(2)}) collective-permute-start(bf16[2,128,512]{2,1,0:T(8,128)(2,1)S(1)} %add_add_fusion.1), channel_id=1, source_target_pairs={{0,2},{8,10},{16,18},{24,26},{1,3},{9,11},{17,19},{25,27}} | collective-permute-start | bytes 786440 | tf_op jit(solution)/shard_map/cond/branch_0_fun/ppermute | solution.py:38
  27.0 1.3 %collective-permute-start.6 = (bf16[2,128,512]{2,1,0:T(8,128)(2,1)S(1)}, bf16[2,128,512]{2,1,0:T(8,128)(2,1)S(1)}, u32[]{:S(2)}, u32[]{:S(2)}) collective-permute-start(bf16[2,128,512]{2,1,0:T(8,128)(2,1)S(1)} %get-tuple-element.57), channel_id=1, source_target_pairs={{0,6},{2,8},{4,10},{6,12},{8,14},{10,16},{12,18},{14,20},{16,22},{... | collective-permute-start | bytes 786440 | tf_op jit(solution)/shard_map/cond/branch_0_fun/ppermute | solution.py:20
  28.3 1.3 %collective-permute-start.7 = (bf16[2,128,512]{2,1,0:T(8,128)(2,1)S(1)}, bf16[2,128,512]{2,1,0:T(8,128)(2,1)S(1)}, u32[]{:S(2)}, u32[]{:S(2)}) collective-permute-start(bf16[2,128,512]{2,1,0:T(8,128)(2,1)S(1)} %get-tuple-element.57), channel_id=1, source_target_pairs={{0,4},{2,6},{4,8},{6,10},{8,12},{10,14},{12,16},{14,18},{16,20},{1... | collective-permute-start | bytes 786440 | tf_op jit(solution)/shard_map/cond/branch_0_fun/ppermute | solution.py:20
  29.6 5.1 %collective-permute-start.8 = (bf16[2,128,512]{2,1,0:T(8,128)(2,1)S(1)}, bf16[2,128,512]{2,1,0:T(8,128)(2,1)S(1)}, u32[]{:S(2)}, u32[]{:S(2)}) collective-permute-start(bf16[2,128,512]{2,1,0:T(8,128)(2,1)S(1)} %get-tuple-element.57), channel_id=1, source_target_pairs={{0,2},{2,4},{4,6},{6,8},{8,10},{10,12},{12,14},{14,16},{16,18},{18... | collective-permute-start | bytes 786440 | tf_op jit(solution)/shard_map/cond/branch_0_fun/ppermute | solution.py:20
  34.8 5.2 %collective-permute-done.7.rest_1_ = bf16[2,128,512]{2,1,0:T(8,128)(2,1)S(1)} collective-permute-done((bf16[2,128,512]{2,1,0:T(8,128)(2,1)S(1)}, bf16[2,128,512]{2,1,0:T(8,128)(2,1)S(1)}, u32[]{:S(2)}, u32[]{:S(2)}) %collective-permute-start.7) | collective-permute-done | bytes 262176 | tf_op jit(solution)/shard_map/cond/branch_0_fun/ppermute | solution.py:20
  40.0 19.2 %tree_attention_1.1 = (bf16[256,4096]{1,0:T(8,128)(2,1)}, bf16[256,4096]{1,0:T(8,128)(2,1)}, f32[2,256,512]{2,1,0:T(8,128)S(1)}, f32[2,128,512]{2,1,0:T(8,128)S(...) custom-call(s32[32]{0:T(128)S(1)} %copy-done.7, ...), custom_call_target="tpu_custom_call" | custom-call | tf_op jit(solution)/shard_map/cond/branch_0_fun/tree_attention_1/pallas_call | solution.py:252
  59.2 1.3 %collective-permute-start.14 = (bf16[2,128,512]{2,1,0:T(8,128)(2,1)S(1)}, bf16[2,128,512]{2,1,0:T(8,128)(2,1)S(1)}, u32[]{:S(2)}, u32[]{:S(2)}) collective-permute-start(bf16[2,128,512]{2,1,0:T(8,128)(2,1)S(1)} %convert_element_type.56), channel_id=1, source_target_pairs={{6,0},{14,8},{22,16},{30,24},{7,1},{15,9},{23,17},{31,25}} | collective-permute-start | bytes 786440 | tf_op jit(solution)/shard_map/cond/branch_0_fun/ppermute | solution.py:54
  60.5 1.3 %collective-permute-start.13 = (bf16[2,128,512]{2,1,0:T(8,128)(2,1)S(1)}, bf16[2,128,512]{2,1,0:T(8,128)(2,1)S(1)}, u32[]{:S(2)}, u32[]{:S(2)}) collective-permute-start(bf16[2,128,512]{2,1,0:T(8,128)(2,1)S(1)} %convert_element_type.56), channel_id=1, source_target_pairs={{4,0},{12,8},{20,16},{28,24},{5,1},{13,9},{21,17},{29,25}} | collective-permute-start | bytes 786440 | tf_op jit(solution)/shard_map/cond/branch_0_fun/ppermute | solution.py:54
  61.8 1.3 %collective-permute-start.12 = (bf16[2,128,512]{2,1,0:T(8,128)(2,1)S(1)}, bf16[2,128,512]{2,1,0:T(8,128)(2,1)S(1)}, u32[]{:S(2)}, u32[]{:S(2)}) collective-permute-start(bf16[2,128,512]{2,1,0:T(8,128)(2,1)S(1)} %convert_element_type.56), channel_id=1, source_target_pairs={{2,0},{10,8},{18,16},{26,24},{3,1},{11,9},{19,17},{27,25}} | collective-permute-start | bytes 786440 | tf_op jit(solution)/shard_map/cond/branch_0_fun/ppermute | solution.py:54
  63.1 1.3 %collective-permute-start.11 = (bf16[2,128,512]{2,1,0:T(8,128)(2,1)S(1)}, bf16[2,128,512]{2,1,0:T(8,128)(2,1)S(1)}, u32[]{:S(2)}, u32[]{:S(2)}) collective-permute-start(bf16[2,128,512]{2,1,0:T(8,128)(2,1)S(1)} %get-tuple-element.33), channel_id=1, source_target_pairs={{6,0},{8,2},{10,4},{12,6},{14,8},{16,10},{18,12},{20,14},{22,16},{... | collective-permute-start | bytes 786440 | tf_op jit(solution)/shard_map/cond/branch_0_fun/ppermute | solution.py:20
  64.4 1.3 %collective-permute-start.10 = (bf16[2,128,512]{2,1,0:T(8,128)(2,1)S(1)}, bf16[2,128,512]{2,1,0:T(8,128)(2,1)S(1)}, u32[]{:S(2)}, u32[]{:S(2)}) collective-permute-start(bf16[2,128,512]{2,1,0:T(8,128)(2,1)S(1)} %get-tuple-element.32), channel_id=1, source_target_pairs={{4,0},{6,2},{8,4},{10,6},{12,8},{14,10},{16,12},{18,14},{20,16},{2... | collective-permute-start | bytes 786440 | tf_op jit(solution)/shard_map/cond/branch_0_fun/ppermute | solution.py:20
  65.7 17.1 %collective-permute-done.14 = bf16[2,128,512]{2,1,0:T(8,128)(2,1)S(1)} collective-permute-done((bf16[2,128,512]{2,1,0:T(8,128)(2,1)S(1)}, bf16[2,128,512]{2,1,0:T(8,128)(2,1)S(1)}, u32[]{:S(2)}, u32[]{:S(2)}) %collective-permute-start.14) | collective-permute-done | bytes 262176 | tf_op jit(solution)/shard_map/cond/branch_0_fun/ppermute | solution.py:54
  82.9 1.3 %collective-permute-start.9 = (bf16[2,128,512]{2,1,0:T(8,128)(2,1)S(1)}, bf16[2,128,512]{2,1,0:T(8,128)(2,1)S(1)}, u32[]{:S(2)}, u32[]{:S(2)}) collective-permute-start(bf16[2,128,512]{2,1,0:T(8,128)(2,1)S(1)} %get-tuple-element.31), channel_id=1, source_target_pairs={{2,0},{4,2},{6,4},{8,6},{10,8},{12,10},{14,12},{16,14},{18,16},{20... | collective-permute-start | bytes 786440 | tf_op jit(solution)/shard_map/cond/branch_0_fun/ppermute | solution.py:20
  84.4 1.3 %collective-permute-start.17 = (bf16[2,128,512]{2,1,0:T(8,128)(2,1)S(1)}, bf16[2,128,512]{2,1,0:T(8,128)(2,1)S(1)}, u32[]{:S(2)}, u32[]{:S(2)}) collective-permute-start(bf16[2,128,512]{2,1,0:T(8,128)(2,1)S(1)} %fusion.6), channel_id=1, source_target_pairs={{24,0},{25,1}} | collective-permute-start | bytes 786440 | tf_op jit(solution)/shard_map/cond/branch_0_fun/ppermute | solution.py:54
  85.7 1.3 %collective-permute-start.16 = (bf16[2,128,512]{2,1,0:T(8,128)(2,1)S(1)}, bf16[2,128,512]{2,1,0:T(8,128)(2,1)S(1)}, u32[]{:S(2)}, u32[]{:S(2)}) collective-permute-start(bf16[2,128,512]{2,1,0:T(8,128)(2,1)S(1)} %fusion.6), channel_id=1, source_target_pairs={{16,0},{17,1}} | collective-permute-start | bytes 786440 | tf_op jit(solution)/shard_map/cond/branch_0_fun/ppermute | solution.py:54
  87.0 1.5 %collective-permute-done.11 = bf16[2,128,512]{2,1,0:T(8,128)(2,1)S(1)} collective-permute-done((bf16[2,128,512]{2,1,0:T(8,128)(2,1)S(1)}, bf16[2,128,512]{2,1,0:T(8,128)(2,1)S(1)}, u32[]{:S(2)}, u32[]{:S(2)}) %collective-permute-start.11) | collective-permute-done | bytes 262176 | tf_op jit(solution)/shard_map/cond/branch_0_fun/ppermute | solution.py:20
  88.5 1.3 %collective-permute-start.15 = (bf16[2,128,512]{2,1,0:T(8,128)(2,1)S(1)}, bf16[2,128,512]{2,1,0:T(8,128)(2,1)S(1)}, u32[]{:S(2)}, u32[]{:S(2)}) collective-permute-start(bf16[2,128,512]{2,1,0:T(8,128)(2,1)S(1)} %fusion.6), channel_id=1, source_target_pairs={{8,0},{9,1}} | collective-permute-start | bytes 786440 | tf_op jit(solution)/shard_map/cond/branch_0_fun/ppermute | solution.py:54
  91.1 11.3 %collective-permute-done.17 = bf16[2,128,512]{2,1,0:T(8,128)(2,1)S(1)} collective-permute-done((bf16[2,128,512]{2,1,0:T(8,128)(2,1)S(1)}, bf16[2,128,512]{2,1,0:T(8,128)(2,1)S(1)}, u32[]{:S(2)}, u32[]{:S(2)}) %collective-permute-start.17) | collective-permute-done | bytes 262176 | tf_op jit(solution)/shard_map/cond/branch_0_fun/ppermute | solution.py:54
  102.4 4.7 %collective-permute-done.16 = bf16[2,128,512]{2,1,0:T(8,128)(2,1)S(1)} collective-permute-done((bf16[2,128,512]{2,1,0:T(8,128)(2,1)S(1)}, bf16[2,128,512]{2,1,0:T(8,128)(2,1)S(1)}, u32[]{:S(2)}, u32[]{:S(2)}) %collective-permute-start.16) | collective-permute-done | bytes 262176 | tf_op jit(solution)/shard_map/cond/branch_0_fun/ppermute | solution.py:54
  108.1 0.8 fusion.5
  (24 shorter events, 2.0 us)
Async XLA Ops:
  3.9 36.1 %copy-start = (bf16[256,512]{1,0:T(8,128)(2,1)S(1)}, bf16[256,512]{1,0:T(8,128)(2,1)}, u32[]{:S(2)}) copy-start(bf16[256,512]{1,0:T(8,128)(2,1)} %get-tuple-element.25.k_own) | copy-start | bytes 786436 | tf_op jit(solution)/shard_map/cond
  3.9 36.1 %copy-start.2 = (bf16[256,512]{1,0:T(8,128)(2,1)S(1)}, bf16[256,512]{1,0:T(8,128)(2,1)}, u32[]{:S(2)}) copy-start(bf16[256,512]{1,0:T(8,128)(2,1)} %get-tuple-element.26.v_own) | copy-start | bytes 786436 | tf_op jit(solution)/shard_map/cond
  3.9 36.1 %copy-start.4 = (bf16[256,4096]{1,0:T(8,128)(2,1)S(1)}, bf16[256,4096]{1,0:T(8,128)(2,1)}, u32[]{:S(2)}) copy-start(bf16[256,4096]{1,0:T(8,128)(2,1)} %get-tuple-element.23.q_ref) | copy-start | bytes 6291460 | tf_op jit(solution)/shard_map/cond
  3.9 36.1 %copy-start.7 = (s32[32]{0:T(128)S(1)}, s32[32]{0:T(128)}, u32[]{:S(2)}) copy-start(s32[32]{0:T(128)} %get-tuple-element.22.parents_ref) | copy-start | bytes 388 | tf_op jit(solution)/shard_map/cond
  6.5 10.8 %collective-permute-start.2 = (bf16[2,128,512]{2,1,0:T(8,128)(2,1)S(1)}, bf16[2,128,512]{2,1,0:T(8,128)(2,1)S(1)}, u32[]{:S(2)}, u32[]{:S(2)}) collective-permute-start(bf16[2,128,512]{2,1,0:T(8,128)(2,1)S(1)} %get-tuple-element.58), channel_id=1, source_target_pairs={{0,24},{1,25}} | collective-permute-start | bytes 786440 | tf_op jit(solution)/shard_map/cond/branch_0_fun/ppermute | solution.py:38
  13.5 6.7 %collective-permute-start.1 = (bf16[2,128,512]{2,1,0:T(8,128)(2,1)S(1)}, bf16[2,128,512]{2,1,0:T(8,128)(2,1)S(1)}, u32[]{:S(2)}, u32[]{:S(2)}) collective-permute-start(bf16[2,128,512]{2,1,0:T(8,128)(2,1)S(1)} %get-tuple-element.58), channel_id=1, source_target_pairs={{0,16},{1,17}} | collective-permute-start | bytes 786440 | tf_op jit(solution)/shard_map/cond/branch_0_fun/ppermute | solution.py:38
  14.8 8.2 %collective-permute-start = (bf16[2,128,512]{2,1,0:T(8,128)(2,1)S(1)}, bf16[2,128,512]{2,1,0:T(8,128)(2,1)S(1)}, u32[]{:S(2)}, u32[]{:S(2)}) collective-permute-start(bf16[2,128,512]{2,1,0:T(8,128)(2,1)S(1)} %get-tuple-element.58), channel_id=1, source_target_pairs={{0,8},{1,9}} | collective-permute-start | bytes 786440 | tf_op jit(solution)/shard_map/cond/branch_0_fun/ppermute | solution.py:38
  23.0 6.6 %collective-permute-start.5 = (bf16[2,128,512]{2,1,0:T(8,128)(2,1)S(1)}, bf16[2,128,512]{2,1,0:T(8,128)(2,1)S(1)}, u32[]{:S(2)}, u32[]{:S(2)}) collective-permute-start(bf16[2,128,512]{2,1,0:T(8,128)(2,1)S(1)} %add_add_fusion.1), channel_id=1, source_target_pairs={{0,6},{8,14},{16,22},{24,30},{1,7},{9,15},{17,23},{25,31}} | collective-permute-start | bytes 786440 | tf_op jit(solution)/shard_map/cond/branch_0_fun/ppermute | solution.py:38
  24.3 10.4 %collective-permute-start.4 = (bf16[2,128,512]{2,1,0:T(8,128)(2,1)S(1)}, bf16[2,128,512]{2,1,0:T(8,128)(2,1)S(1)}, u32[]{:S(2)}, u32[]{:S(2)}) collective-permute-start(bf16[2,128,512]{2,1,0:T(8,128)(2,1)S(1)} %add_add_fusion.1), channel_id=1, source_target_pairs={{0,4},{8,12},{16,20},{24,28},{1,5},{9,13},{17,21},{25,29}} | collective-permute-start | bytes 786440 | tf_op jit(solution)/shard_map/cond/branch_0_fun/ppermute | solution.py:38
  25.7 9.1 %collective-permute-start.3 = (bf16[2,128,512]{2,1,0:T(8,128)(2,1)S(1)}, bf16[2,128,512]{2,1,0:T(8,128)(2,1)S(1)}, u32[]{:S(2)}, u32[]{:S(2)}) collective-permute-start(bf16[2,128,512]{2,1,0:T(8,128)(2,1)S(1)} %add_add_fusion.1), channel_id=1, source_target_pairs={{0,2},{8,10},{16,18},{24,26},{1,3},{9,11},{17,19},{25,27}} | collective-permute-start | bytes 786440 | tf_op jit(solution)/shard_map/cond/branch_0_fun/ppermute | solution.py:38
  27.0 7.9 %collective-permute-start.6 = (bf16[2,128,512]{2,1,0:T(8,128)(2,1)S(1)}, bf16[2,128,512]{2,1,0:T(8,128)(2,1)S(1)}, u32[]{:S(2)}, u32[]{:S(2)}) collective-permute-start(bf16[2,128,512]{2,1,0:T(8,128)(2,1)S(1)} %get-tuple-element.57), channel_id=1, source_target_pairs={{0,6},{2,8},{4,10},{6,12},{8,14},{10,16},{12,18},{14,20},{16,22},{... | collective-permute-start | bytes 786440 | tf_op jit(solution)/shard_map/cond/branch_0_fun/ppermute | solution.py:20
  28.3 11.7 %collective-permute-start.7 = (bf16[2,128,512]{2,1,0:T(8,128)(2,1)S(1)}, bf16[2,128,512]{2,1,0:T(8,128)(2,1)S(1)}, u32[]{:S(2)}, u32[]{:S(2)}) collective-permute-start(bf16[2,128,512]{2,1,0:T(8,128)(2,1)S(1)} %get-tuple-element.57), channel_id=1, source_target_pairs={{0,4},{2,6},{4,8},{6,10},{8,12},{10,14},{12,16},{14,18},{16,20},{1... | collective-permute-start | bytes 786440 | tf_op jit(solution)/shard_map/cond/branch_0_fun/ppermute | solution.py:20
  29.6 10.4 %collective-permute-start.8 = (bf16[2,128,512]{2,1,0:T(8,128)(2,1)S(1)}, bf16[2,128,512]{2,1,0:T(8,128)(2,1)S(1)}, u32[]{:S(2)}, u32[]{:S(2)}) collective-permute-start(bf16[2,128,512]{2,1,0:T(8,128)(2,1)S(1)} %get-tuple-element.57), channel_id=1, source_target_pairs={{0,2},{2,4},{4,6},{6,8},{8,10},{10,12},{12,14},{14,16},{16,18},{18... | collective-permute-start | bytes 786440 | tf_op jit(solution)/shard_map/cond/branch_0_fun/ppermute | solution.py:20
  59.2 23.6 %collective-permute-start.14 = (bf16[2,128,512]{2,1,0:T(8,128)(2,1)S(1)}, bf16[2,128,512]{2,1,0:T(8,128)(2,1)S(1)}, u32[]{:S(2)}, u32[]{:S(2)}) collective-permute-start(bf16[2,128,512]{2,1,0:T(8,128)(2,1)S(1)} %convert_element_type.56), channel_id=1, source_target_pairs={{6,0},{14,8},{22,16},{30,24},{7,1},{15,9},{23,17},{31,25}} | collective-permute-start | bytes 786440 | tf_op jit(solution)/shard_map/cond/branch_0_fun/ppermute | solution.py:54
  60.5 23.6 %collective-permute-start.13 = (bf16[2,128,512]{2,1,0:T(8,128)(2,1)S(1)}, bf16[2,128,512]{2,1,0:T(8,128)(2,1)S(1)}, u32[]{:S(2)}, u32[]{:S(2)}) collective-permute-start(bf16[2,128,512]{2,1,0:T(8,128)(2,1)S(1)} %convert_element_type.56), channel_id=1, source_target_pairs={{4,0},{12,8},{20,16},{28,24},{5,1},{13,9},{21,17},{29,25}} | collective-permute-start | bytes 786440 | tf_op jit(solution)/shard_map/cond/branch_0_fun/ppermute | solution.py:54
  61.8 22.3 %collective-permute-start.12 = (bf16[2,128,512]{2,1,0:T(8,128)(2,1)S(1)}, bf16[2,128,512]{2,1,0:T(8,128)(2,1)S(1)}, u32[]{:S(2)}, u32[]{:S(2)}) collective-permute-start(bf16[2,128,512]{2,1,0:T(8,128)(2,1)S(1)} %convert_element_type.56), channel_id=1, source_target_pairs={{2,0},{10,8},{18,16},{26,24},{3,1},{11,9},{19,17},{27,25}} | collective-permute-start | bytes 786440 | tf_op jit(solution)/shard_map/cond/branch_0_fun/ppermute | solution.py:54
  63.1 25.4 %collective-permute-start.11 = (bf16[2,128,512]{2,1,0:T(8,128)(2,1)S(1)}, bf16[2,128,512]{2,1,0:T(8,128)(2,1)S(1)}, u32[]{:S(2)}, u32[]{:S(2)}) collective-permute-start(bf16[2,128,512]{2,1,0:T(8,128)(2,1)S(1)} %get-tuple-element.33), channel_id=1, source_target_pairs={{6,0},{8,2},{10,4},{12,6},{14,8},{16,10},{18,12},{20,14},{22,16},{... | collective-permute-start | bytes 786440 | tf_op jit(solution)/shard_map/cond/branch_0_fun/ppermute | solution.py:20
  64.4 26.7 %collective-permute-start.10 = (bf16[2,128,512]{2,1,0:T(8,128)(2,1)S(1)}, bf16[2,128,512]{2,1,0:T(8,128)(2,1)S(1)}, u32[]{:S(2)}, u32[]{:S(2)}) collective-permute-start(bf16[2,128,512]{2,1,0:T(8,128)(2,1)S(1)} %get-tuple-element.32), channel_id=1, source_target_pairs={{4,0},{6,2},{8,4},{10,6},{12,8},{14,10},{16,12},{18,14},{20,16},{2... | collective-permute-start | bytes 786440 | tf_op jit(solution)/shard_map/cond/branch_0_fun/ppermute | solution.py:20
  82.9 8.2 %collective-permute-start.9 = (bf16[2,128,512]{2,1,0:T(8,128)(2,1)S(1)}, bf16[2,128,512]{2,1,0:T(8,128)(2,1)S(1)}, u32[]{:S(2)}, u32[]{:S(2)}) collective-permute-start(bf16[2,128,512]{2,1,0:T(8,128)(2,1)S(1)} %get-tuple-element.31), channel_id=1, source_target_pairs={{2,0},{4,2},{6,4},{8,6},{10,8},{12,10},{14,12},{16,14},{18,16},{20... | collective-permute-start | bytes 786440 | tf_op jit(solution)/shard_map/cond/branch_0_fun/ppermute | solution.py:20
  84.4 18.0 %collective-permute-start.17 = (bf16[2,128,512]{2,1,0:T(8,128)(2,1)S(1)}, bf16[2,128,512]{2,1,0:T(8,128)(2,1)S(1)}, u32[]{:S(2)}, u32[]{:S(2)}) collective-permute-start(bf16[2,128,512]{2,1,0:T(8,128)(2,1)S(1)} %fusion.6), channel_id=1, source_target_pairs={{24,0},{25,1}} | collective-permute-start | bytes 786440 | tf_op jit(solution)/shard_map/cond/branch_0_fun/ppermute | solution.py:54
  85.7 21.4 %collective-permute-start.16 = (bf16[2,128,512]{2,1,0:T(8,128)(2,1)S(1)}, bf16[2,128,512]{2,1,0:T(8,128)(2,1)S(1)}, u32[]{:S(2)}, u32[]{:S(2)}) collective-permute-start(bf16[2,128,512]{2,1,0:T(8,128)(2,1)S(1)} %fusion.6), channel_id=1, source_target_pairs={{16,0},{17,1}} | collective-permute-start | bytes 786440 | tf_op jit(solution)/shard_map/cond/branch_0_fun/ppermute | solution.py:54
  88.5 19.1 %collective-permute-start.15 = (bf16[2,128,512]{2,1,0:T(8,128)(2,1)S(1)}, bf16[2,128,512]{2,1,0:T(8,128)(2,1)S(1)}, u32[]{:S(2)}, u32[]{:S(2)}) collective-permute-start(bf16[2,128,512]{2,1,0:T(8,128)(2,1)S(1)} %fusion.6), channel_id=1, source_target_pairs={{8,0},{9,1}} | collective-permute-start | bytes 786440 | tf_op jit(solution)/shard_map/cond/branch_0_fun/ppermute | solution.py:54
where the time goes:
time: 109 us
  waiting for transfers between devices  47.2 us (43%)
  starting transfers between devices  32.8 us (30%)
  Pallas kernels  21.2 us (19%)
  other arithmetic  2.83 us (3%)
  loops' own time  2.42 us (2%)
  between operations  1.29 us (1%)
  local copies, waits for them, and re-layouts  1.19 us (1%)
    ppermute x6, waiting for transfers between devices, sum_to_first(): lax.ppermute(sent, 'ctx', [(i + j * stride, i) for i in range(0, devices,...  33.6 us
    pallas_call x1, Pallas kernels, attention(): pl.pallas_call(functools.partial(attention_kernel, carried, blocks_here,...  19.2 us
    ppermute x6, starting transfers between devices, spread_from_first(): lax.ppermute(held, 'ctx', [(i, i + j * stride) for i in range(0, devices,...  13.5 us
    ppermute x6, starting transfers between devices, passed_along(): return lax.ppermute(array, 'ctx', pairs)  11.6 us
    ppermute x6, starting transfers between devices, sum_to_first(): lax.ppermute(sent, 'ctx', [(i + j * stride, i) for i in range(0, devices,...  7.74 us
    ppermute x6, waiting for transfers between devices, spread_from_first(): lax.ppermute(held, 'ctx', [(i, i + j * stride) for i in range(0, devices,...  6.85 us
    ppermute x6, waiting for transfers between devices, passed_along(): return lax.ppermute(array, 'ctx', pairs)  6.72 us
    another operation x1, loops' own time, local(): lax.cond(choice[-1] > 1, functools.partial(run, blocks_here), functools.p...  2.42 us
  transfers between devices with their start and end apart: 18, of which 9 were waited for; matrix products, arithmetic and copies ran while one was open for 0% of the time, Pallas kernels for 0%

commit v1 on v0

v1 whole, which is shorter than its diff:
```python
import functools
import math

import jax
import jax.numpy as jnp
from jax import lax
from jax.experimental import pallas as pl
from jax.experimental.pallas import tpu as pltpu
from jax.sharding import PartitionSpec as P

HEAD_WIDTH = 128
BLOCK_TOKENS = 128
HOPS = 3
LAYER = 4


def passed_along(array, by):
    devices = lax.axis_size("ctx")
    pairs = [(i, i + by) for i in range(devices) if 0 <= i + by < devices]
    return lax.ppermute(array, "ctx", pairs)


def layer_stages(layers):
    stages = []
    while layers > 1:
        fan = 4 if layers % 4 == 0 else (2 if layers % 2 == 0 else layers)
        layers //= fan
        stages.append((layers, fan))
    return stages


def spread_from_first(held, after=()):
    devices = lax.axis_size("ctx")
    position = lax.axis_index("ctx")
    layers = devices // LAYER
    layer = position // LAYER
    for stride, fan in layer_stages(layers):
        bases = range(0, layers, stride * fan)
        arrived = [
            lax.ppermute(held, "ctx", [(b * LAYER, (b + j * stride) * LAYER) for b in bases])
            for j in range(1, fan)
        ]
        held, *arrived = lax.optimization_barrier((held, *arrived))
        for j, piece in enumerate(arrived, 1):
            here = (position % LAYER == 0) & (layer % (stride * fan) == j * stride)
            held = jnp.where(here, piece, held)
    held, *after = lax.optimization_barrier((held, *after))
    for step in (2, 1):
        pairs = [(i, i + step) for i in range(0, devices, 2 * step)]
        here = (position % (2 * step)) == step
        held = jnp.where(here, lax.ppermute(held, "ctx", pairs), held)
    return (held, *after)


def sum_to_first(total, after=()):
    devices = lax.axis_size("ctx")
    layers = devices // LAYER
    home = lambda layer: layer * LAYER + (2 if layer else 0)
    stages = [[[(i + 1, i) for i in range(0, devices, 2)]]]
    stages.append([[(home(l) ^ 2, home(l)) for l in range(layers)]])
    for stride, fan in reversed(layer_stages(layers)):
        bases = range(0, layers, stride * fan)
        stages.append(
            [[(home(b + j * stride), home(b)) for b in bases] for j in range(1, fan)]
        )
    for at, stage in enumerate(stages):
        sent = total.astype(jnp.bfloat16)
        arrived = [lax.ppermute(sent, "ctx", pairs) for pairs in stage]
        if at == 0:
            arrived[0], *after = lax.optimization_barrier((arrived[0], *after))
        for piece in arrived:
            total = total + piece.astype(jnp.float32)
    return (total, *after)


def export_kernel(
    blocks_here, parents_ref, k_ref, v_ref, choice_ref, crowded_ref, first_ref, sent_ref, reach_ref
):
    block_count = parents_ref.shape[0]
    for b in range(block_count):
        reach_ref[b] = jnp.int32(b // blocks_here)
    crowded = jnp.int32(0)
    for device in reversed(range(block_count // blocks_here)):
        count = jnp.int32(0)
        choice = jnp.int32(0)
        for slot in reversed(range(blocks_here)):
            block = device * blocks_here + slot
            if block == 0:
                continue
            last = reach_ref[block]
            up = parents_ref[block]
            reach_ref[up] = jnp.maximum(reach_ref[up], last)
            read = last > device
            count = count + read.astype(jnp.int32)
            choice = jnp.where(read, slot, choice)
        choice_ref[device] = choice
        crowded = jnp.maximum(crowded, count)
    crowded_ref[0] = crowded
    mine = choice_ref[lax.axis_index("ctx")]
    rows = pl.ds(pl.multiple_of(mine * BLOCK_TOKENS, BLOCK_TOKENS), BLOCK_TOKENS)
    for which, ref in enumerate((k_ref, v_ref)):
        first_ref[which] = ref[:BLOCK_TOKENS]
        sent_ref[which] = ref[rows]


def exported_blocks(parents, key, value):
    blocks_here = key.shape[0] // BLOCK_TOKENS
    block_count = parents.shape[0]
    smem = pl.BlockSpec(memory_space=pltpu.SMEM)
    vmem = pl.BlockSpec(memory_space=pltpu.VMEM)
    pair = jax.ShapeDtypeStruct((2, BLOCK_TOKENS, key.shape[1]), key.dtype)
    return pl.pallas_call(
        functools.partial(export_kernel, blocks_here),
        out_shape=[
            jax.ShapeDtypeStruct((block_count // blocks_here,), jnp.int32),
            jax.ShapeDtypeStruct((1,), jnp.int32),
            pair,
            pair,
        ],
        in_specs=[smem, vmem, vmem],
        out_specs=[smem, smem, vmem, vmem],
        scratch_shapes=[pltpu.SMEM((block_count,), jnp.int32)],
        name="exported",
    )(parents, key, value)


NT = (((1,), (1,)), ((), ()))
NN = (((1,), (0,)), ((), ()))
TN = (((0,), (0,)), ((), ()))


def dot(a, b, dims):
    return lax.dot_general(a, b, dims, preferred_element_type=jnp.float32)


def attention_kernel(
    plan, blocks_here, heads_per_group, parents_ref, q_ref, do_ref, k_own, v_own, root_ref, *rest
):
    held_counts, slot_of, chunk_heads, sub_heads, skew = plan
    arrivals = rest[: len(held_counts)]
    (out_ref, gq_ref, gown_ref, groot_ref) = rest[len(held_counts) : len(held_counts) + 4]
    departures = rest[len(held_counts) + 4 : 2 * len(held_counts) + 4]
    k_all, v_all, gk_acc, gv_acc, slots, counts = rest[2 * len(held_counts) + 4 :]
    own_base = 1 + sum(held_counts)
    scale = 1.0 / math.sqrt(HEAD_WIDTH)
    log2e = math.log2(math.e)
    rows = sub_heads * BLOCK_TOKENS
    most_seen = slots.shape[1]

    @pl.when(pl.program_id(0) == 0)
    def _():
        position = lax.axis_index("ctx")
        for qb in range(blocks_here):
            own = position * blocks_here + qb
            slots[qb, 0] = 0

            def climb(step, state):
                current, count = state
                current = parents_ref[current]
                device = lax.div(current, blocks_here)
                slot = lax.rem(current, blocks_here)
                back = position - device
                where_held = jnp.where(back == 0, own_base + slot, slot_of(position, back, slot))
                seen = (current > 0) & (back <= HOPS)

                @pl.when(seen)
                def _():
                    slots[qb, count] = where_held

                return current, count + seen.astype(jnp.int32)

            _, count = lax.fori_loop(
                0, (HOPS + 1) * blocks_here, climb, (own, jnp.int32(1))
            )

            @pl.when(own > 0)
            def _():
                slots[qb, count] = own_base + qb

            counts[qb] = jnp.where(own > 0, count + 1, 1)

    k_all[0] = root_ref[0]
    v_all[0] = root_ref[1]
    at = 1
    for arrival, count in zip(arrivals, held_counts):
        for e in range(count):
            part = slice(e * BLOCK_TOKENS, (e + 1) * BLOCK_TOKENS)
            k_all[at] = arrival[0, part]
            v_all[at] = arrival[1, part]
            at += 1
    for b in range(blocks_here):
        k_all[own_base + b] = k_own[b * BLOCK_TOKENS : (b + 1) * BLOCK_TOKENS]
        v_all[own_base + b] = v_own[b * BLOCK_TOKENS : (b + 1) * BLOCK_TOKENS]
    gk_acc[...] = jnp.zeros_like(gk_acc)
    gv_acc[...] = jnp.zeros_like(gv_acc)

    def run_block(qb, seen):
        held = [slots[qb, j] for j in range(seen)]
        tokens = pl.ds(pl.multiple_of(qb * BLOCK_TOKENS, BLOCK_TOKENS), BLOCK_TOKENS)

        keys = jnp.concatenate([k_all[s] for s in held], axis=0)
        values = jnp.concatenate([v_all[s] for s in held], axis=0)
        split = lambda wide: [
            wide[:, j * BLOCK_TOKENS : (j + 1) * BLOCK_TOKENS] for j in range(seen)
        ]

        def run_chunk(chunk, carry):
            def load(ref, sub):
                return jnp.concatenate([ref[tokens, c] for c in columns(sub)], axis=0)

            def columns(sub):
                return [
                    pl.ds(
                        pl.multiple_of((chunk * chunk_heads + sub * sub_heads + h) * HEAD_WIDTH, HEAD_WIDTH),
                        HEAD_WIDTH,
                    )
                    for h in range(sub_heads)
                ]

            def first(sub):
                q, do = load(q_ref, sub), load(do_ref, sub)
                return dot(q, keys, NT), dot(do, values, NT)

            def second(sub, scores, gprobs):
                scores = split(scores)
                token = lax.broadcasted_iota(jnp.int32, (rows, BLOCK_TOKENS), 0) % BLOCK_TOKENS
                other = lax.broadcasted_iota(jnp.int32, (rows, BLOCK_TOKENS), 1)
                scores[-1] = jnp.where(other <= token, scores[-1], -jnp.inf)
                top = functools.reduce(jnp.maximum, scores)
                top = jnp.max(top, axis=1, keepdims=True) * (scale * log2e)
                raised = [jnp.exp2(s * (scale * log2e) - top) for s in scores]
                total = jnp.sum(functools.reduce(jnp.add, raised), axis=1, keepdims=True)
                inverse = 1.0 / total
                probs = [r * inverse for r in raised]
                weights = jnp.concatenate([p.astype(jnp.bfloat16) for p in probs], axis=1)
                attended = dot(weights, values, NN).astype(jnp.bfloat16)
                for h, c in enumerate(columns(sub)):
                    out_ref[tokens, c] = attended[h * BLOCK_TOKENS : (h + 1) * BLOCK_TOKENS]
                return probs, weights, attended, gprobs

            def third(sub, probs, weights, attended, gprobs):
                q, do = load(q_ref, sub), load(do_ref, sub)
                delta = jnp.sum(
                    do.astype(jnp.float32) * attended.astype(jnp.float32), axis=1, keepdims=True
                )
                dscores = jnp.concatenate(
                    [(p * (g - delta)).astype(jnp.bfloat16) for p, g in zip(probs, split(gprobs))],
                    axis=1,
                )
                grad_q = (dot(dscores, keys, NN) * scale).astype(jnp.bfloat16)
                for h, c in enumerate(columns(sub)):
                    gq_ref[tokens, c] = grad_q[h * BLOCK_TOKENS : (h + 1) * BLOCK_TOKENS]
                gk = split(dot(q, dscores, TN))
                gv = split(dot(do, weights, TN))
                for s, x, y in zip(held, gk, gv):
                    gk_acc[s] += x
                    gv_acc[s] += y

            subs = chunk_heads // sub_heads
            one, two = {}, {}
            for turn in range(subs + 2 * skew):
                if turn < subs:
                    one[turn] = first(turn)
                if 0 <= turn - skew < subs:
                    two[turn - skew] = second(turn - skew, *one.pop(turn - skew))
                if 0 <= turn - 2 * skew < subs:
                    third(turn - 2 * skew, *two.pop(turn - 2 * skew))
            return carry

        lax.fori_loop(0, heads_per_group // chunk_heads, run_chunk, 0)

    @pl.loop(0, blocks_here)
    def _(qb):
        seen_here = counts[qb]
        for seen in range(1, most_seen + 1):
            pl.when(seen_here == seen)(functools.partial(run_block, qb, seen))

    def grads(slot):
        return (gk_acc[slot] * scale).T, gv_acc[slot].T

    for b in range(blocks_here):
        part = slice(b * BLOCK_TOKENS, (b + 1) * BLOCK_TOKENS)
        gown_ref[0, part], gown_ref[1, part] = grads(own_base + b)
    groot_ref[0], groot_ref[1] = grads(0)
    at = 1
    for departure, count in zip(departures, held_counts):
        for e in range(count):
            part = slice(e * BLOCK_TOKENS, (e + 1) * BLOCK_TOKENS)
            gk, gv = grads(at)
            departure[0, part] = gk.astype(jnp.bfloat16)
            departure[1, part] = gv.astype(jnp.bfloat16)
            at += 1


def attention(plan, most_seen, parents, query, grad, key, value, root_pair, arrivals):
    tokens_here = query.shape[0]
    blocks_here = tokens_here // BLOCK_TOKENS
    groups = key.shape[1] // HEAD_WIDTH
    heads_per_group = query.shape[1] // HEAD_WIDTH // groups
    wide = pl.BlockSpec((tokens_here, heads_per_group * HEAD_WIDTH), lambda g, _: (0, g))
    narrow = pl.BlockSpec((tokens_here, HEAD_WIDTH), lambda g, _: (0, g))
    pair = lambda rows: pl.BlockSpec((2, rows, HEAD_WIDTH), lambda g, _: (0, 0, g))
    arrival_specs = [pair(a.shape[1]) for a in arrivals]
    slot_count = 1 + sum(plan[0]) + blocks_here
    like = lambda array, kind: jax.ShapeDtypeStruct(array.shape, kind)
    blocks = pltpu.VMEM((slot_count, BLOCK_TOKENS, HEAD_WIDTH), jnp.bfloat16)
    sums = pltpu.VMEM((slot_count, HEAD_WIDTH, BLOCK_TOKENS), jnp.float32)
    return pl.pallas_call(
        functools.partial(attention_kernel, plan, blocks_here, heads_per_group),
        grid_spec=pltpu.PrefetchScalarGridSpec(
            num_scalar_prefetch=1,
            grid=(groups,),
            in_specs=[wide, wide, narrow, narrow, pair(BLOCK_TOKENS)] + arrival_specs,
            out_specs=[wide, wide, pair(tokens_here), pair(BLOCK_TOKENS)] + arrival_specs,
            scratch_shapes=[
                blocks,
                blocks,
                sums,
                sums,
                pltpu.SMEM((blocks_here, most_seen), jnp.int32),
                pltpu.SMEM((blocks_here,), jnp.int32),
            ],
        ),
        out_shape=[
            like(query, jnp.bfloat16),
            like(query, jnp.bfloat16),
            jax.ShapeDtypeStruct((2,) + key.shape, jnp.float32),
            like(root_pair, jnp.float32),
        ]
        + [like(a, jnp.bfloat16) for a in arrivals],
        compiler_params=pltpu.CompilerParams(vmem_limit_bytes=48 << 20),
        name=f"tree_attention_{most_seen}",
    )(parents, query, grad, key, value, root_pair, *arrivals)


def wide32(array):
    return array.astype(jnp.float32)


def run_every_block(choice, first, sent, query, key, value, output_cotangent, parents):
    blocks_here = query.shape[0] // BLOCK_TOKENS
    position = lax.axis_index("ctx")
    key_value = jnp.stack([key, value])
    (root_pair,) = spread_from_first(first)
    pieces = [passed_along(key_value, back) for back in range(HOPS, 0, -1)]
    slot_of = lambda position, back, slot: 1 + (HOPS - back) * blocks_here + slot
    plan = ((blocks_here,) * HOPS, slot_of, 2, 2, 0)
    out, grad_q, own, root_terms, *terms = attention(
        plan, 1 + (HOPS + 1) * blocks_here, parents, query, output_cotangent, key, value,
        root_pair, pieces,
    )
    total = own + sum(
        wide32(passed_along(terms[HOPS - back], -back)) for back in range(1, HOPS + 1)
    )
    root_rows = jnp.where(position == 0, sum_to_first(root_terms)[0], 0.0)
    total = jnp.concatenate(
        [total[:, :BLOCK_TOKENS] + root_rows, total[:, BLOCK_TOKENS:]], axis=1
    ).astype(jnp.bfloat16)
    return out, grad_q, total[0], total[1]


def run_one_block(choice, first, sent, query, key, value, output_cotangent, parents):
    blocks_here = query.shape[0] // BLOCK_TOKENS
    devices = lax.axis_size("ctx")
    position = lax.axis_index("ctx")
    odd = position % 2
    swap = [(i, i ^ 1) for i in range(devices)]
    skip = [(i, i + 3) for i in range(1, devices - 3, 2)]
    mine = choice[position]
    two_back = passed_along(sent, 2)
    three_back = lax.ppermute(sent, "ctx", skip)
    root_pair, two_back, three_back = spread_from_first(first, (two_back, three_back))
    across = lax.ppermute(jnp.concatenate([two_back, sent], axis=1), "ctx", swap)

    def slot_of(position, back, slot):
        odd = lax.rem(position, 2)
        return jnp.where(back == 2, 2, jnp.where(back == 1, 3 + odd, 1 + 2 * odd))

    plan = ((1, 1, 2), slot_of, 8, 2, 1)
    out, grad_q, own, root_terms, g_three, g_two, g_across = attention(
        plan, 1 + HOPS + blocks_here, parents, query, output_cotangent, key, value, root_pair,
        [three_back, two_back, across],
    )
    from_core = lax.ppermute(g_across, "ctx", swap)
    from_three = lax.ppermute(g_three, "ctx", [(b, a) for a, b in skip])
    root_sum, from_core = sum_to_first(root_terms, (from_core,))
    merged = wide32(g_two) + wide32(from_core[:, :BLOCK_TOKENS])
    from_two = passed_along(merged.astype(jnp.bfloat16), -2)

    block = lax.broadcasted_iota(jnp.int32, (blocks_here, BLOCK_TOKENS, key.shape[1]), 0)
    at_first = (block == 0) & (position == 0)

    def final(which):
        returned = (
            wide32(from_two[which]) + wide32(from_three[which])
            + jnp.where(odd == 0, wide32(from_core[which, BLOCK_TOKENS:]), 0.0)
        )
        total = own[which].reshape(block.shape)
        total = total + jnp.where(block == mine, returned[None], 0.0)
        total = total + jnp.where(at_first, root_sum[which][None], 0.0)
        return total.astype(jnp.bfloat16).reshape(key.shape)

    return out, grad_q, final(0), final(1)


def local(query, key, value, output_cotangent, parents):
    choice, crowded, first, sent = exported_blocks(parents, key, value)
    return lax.cond(
        crowded[0] > 1,
        run_every_block,
        run_one_block,
        choice, first, sent, query, key, value, output_cotangent, parents,
    )


def solution(mesh):
    in_specs = (P("ctx", "tp"), P("ctx", "tp"), P("ctx", "tp"), P("ctx", "tp"), P())
    out_specs = (P("ctx", "tp"), P("ctx", "tp"), P("ctx", "tp"), P("ctx", "tp"))
    return jax.shard_map(local, mesh=mesh, in_specs=in_specs, out_specs=out_specs, check_vma=False)
```

time: 109 us -> 85.9 us (0.79)
  waiting for transfers between devices: 47.2 us -> 34.6 us
  starting transfers between devices: 32.8 us -> 23.7 us
  other arithmetic: 2.83 us -> 5.8 us
  Pallas kernels: 21.2 us -> 18.3 us
  loops' own time: 2.42 us -> 0.3 us
    ppermute x6 -> x2, starting transfers between devices: 11.6 us -> 2.59 us  [passed_along(): return lax.ppermute(array, 'ctx', pairs)]
    ppermute x12 -> x14, waiting for transfers between devices: 40.5 us -> 32.8 us  [the longest x5 21.1 us: sum_to_first(): arrived = [lax.ppermute(sent, 'ctx', pairs) for pairs in stage]]
    ppermute x6 -> x2, waiting for transfers between devices: 6.72 us -> 1.84 us  [passed_along(): return lax.ppermute(array, 'ctx', pairs)]
    pallas_call x2, Pallas kernels: 21.2 us -> 18.3 us  [the longest x1 16.5 us: attention(): pl.pallas_call(functools.partial(attention_kernel, plan, blocks_here, hea...]
    another operation x1, loops' own time: 2.42 us -> 0.3 us  [local(): lax.cond(crowded[0] > 1, run_every_block, run_one_block, choice, first, s...]
    convert_element_type x0 -> x2, other arithmetic: none -> 1.87 us  [the longest x1 1.09 us: final(): return total.astype(jnp.bfloat16).reshape(key.shape)]
    another operation x2 -> x0, other arithmetic: 1.69 us -> none  [the longest x1 1.15 us: run(): key_value = jnp.stack([key, value])]
    ppermute x12 -> x14, starting transfers between devices: 21.2 us -> 21.1 us  [the longest x3 8.32 us: spread_from_first(): lax.ppermute(held, 'ctx', [(b * LAYER, (b + j * stride) * LAYER) for b in...]
  transfers between devices with their start and end apart: 18 -> 16, of which waited for: 9 -> 10; matrix products, arithmetic and copies ran while one was open for 0% -> 5% of each run, Pallas kernels for 0% -> 0%
where the time goes in v1:
time: 85.9 us; the launch traced here: 85.4 us
  waiting for transfers between devices  34.6 us (40%)
  starting transfers between devices  23.7 us (28%)
  Pallas kernels  18.3 us (21%)
  other arithmetic  5.8 us (7%)
  local copies, waits for them, and re-layouts  1.4 us (2%)
  between operations  1.29 us (2%)
    ppermute x5, waiting for transfers between devices, sum_to_first(): arrived = [lax.ppermute(sent, 'ctx', pairs) for pairs in stage]  21.1 us
    pallas_call x1, Pallas kernels, attention(): pl.pallas_call(functools.partial(attention_kernel, plan, blocks_here, hea...  16.5 us
    ppermute x3, starting transfers between devices, spread_from_first(): lax.ppermute(held, 'ctx', [(b * LAYER, (b + j * stride) * LAYER) for b in...  8.32 us
    ppermute x3, waiting for transfers between devices, spread_from_first(): lax.ppermute(held, 'ctx', [(b * LAYER, (b + j * stride) * LAYER) for b in...  6.83 us
    ppermute x5, starting transfers between devices, sum_to_first(): arrived = [lax.ppermute(sent, 'ctx', pairs) for pairs in stage]  6.45 us
    ppermute x2, waiting for transfers between devices, spread_from_first(): held = jnp.where(here, lax.ppermute(held, 'ctx', pairs), held)  4.84 us
    ppermute x2, starting transfers between devices, spread_from_first(): held = jnp.where(here, lax.ppermute(held, 'ctx', pairs), held)  2.61 us
    ppermute x2, starting transfers between devices, passed_along(): return lax.ppermute(array, 'ctx', pairs)  2.59 us
  transfers between devices with their start and end apart: 16, of which 10 were waited for; matrix products, arithmetic and copies ran while one was open for 5% of the time, Pallas kernels for 0%

profile of v1, /device:TPU:0, one launch (start us, length us, event | category | flops | bytes accessed | tf_op | source)
XLA Modules:
  0.0 85.4 jit_solution(14000059393398020799)
XLA Ops:
  0.6 1.8 %exported.1 = (s32[16]{0:T(128)S(1)}, s32[1]{0:T(128)}, bf16[2,128,512]{2,1,0:T(8,128)(2,1)S(1)}, bf16[2,128,512]{2,1,0:T(8,128)(2,1)S(1)}) custom-call(s32[32]{0:T(128)} %parents_ref.1, bf16[256,512]{1,0:T(8,128)(2,1)} %k_ref.1, bf16[256,512]{1,0:T(8,128)(2,1)} %v_ref.1), custom_call_target="tpu_custom_call" | custom-call | tf_op jit(solution)/shard_map/exported/pallas_call | solution.py:112
  3.1 82.3 %conditional.1 = (bf16[256,4096]{1,0:T(8,128)(2,1)}, bf16[256,4096]{1,0:T(8,128)(2,1)}, bf16[256,512]{1,0:T(8,128)(2,1)}, bf16[256,512]{1,0:T(8,128)(2,1)}) conditional(s32[]{:T(128)} %bitcast.17, (bf16[2,128,512]{2,1,0:T(8,128)(2,1)S(1)}, bf16[2,128,512]{2,1,0:T(8,128)(2,1)S(1)}, s32[32]{0:T(128)}, bf16[256,4096]{1,0:T(8,128)(2,1)}, ...), branch_computations={%region_0.1_spmd, %region_1.2_spmd} | conditional | flops 6815804 | bytes 39061180 | solution.py:408
  3.1 4.9 %collective-permute-start = (bf16[2,128,512]{2,1,0:T(8,128)(2,1)S(1)}, bf16[2,128,512]{2,1,0:T(8,128)(2,1)S(1)}, u32[]{:S(2)}, u32[]{:S(2)}) collective-permute-start(bf16[2,128,512]{2,1,0:T(8,128)(2,1)S(1)} %get-tuple-element.37), channel_id=1, source_target_pairs={{0,8},{1,9}} | collective-permute-start | bytes 786440 | tf_op jit(solution)/shard_map/cond/branch_0_fun/ppermute | solution.py:40
  8.1 1.7 %collective-permute-start.1 = (bf16[2,128,512]{2,1,0:T(8,128)(2,1)S(1)}, bf16[2,128,512]{2,1,0:T(8,128)(2,1)S(1)}, u32[]{:S(2)}, u32[]{:S(2)}) collective-permute-start(bf16[2,128,512]{2,1,0:T(8,128)(2,1)S(1)} %get-tuple-element.37), channel_id=1, source_target_pairs={{0,16},{1,17}} | collective-permute-start | bytes 786440 | tf_op jit(solution)/shard_map/cond/branch_0_fun/ppermute | solution.py:40
  9.8 1.7 %collective-permute-start.2 = (bf16[2,128,512]{2,1,0:T(8,128)(2,1)S(1)}, bf16[2,128,512]{2,1,0:T(8,128)(2,1)S(1)}, u32[]{:S(2)}, u32[]{:S(2)}) collective-permute-start(bf16[2,128,512]{2,1,0:T(8,128)(2,1)S(1)} %get-tuple-element.37), channel_id=1, source_target_pairs={{0,24},{1,25}} | collective-permute-start | bytes 786440 | tf_op jit(solution)/shard_map/cond/branch_0_fun/ppermute | solution.py:40
  11.5 1.3 %collective-permute-start.3 = (bf16[2,128,512]{2,1,0:T(8,128)(2,1)S(1)}, bf16[2,128,512]{2,1,0:T(8,128)(2,1)S(1)}, u32[]{:S(2)}, u32[]{:S(2)}) collective-permute-start(bf16[2,128,512]{2,1,0:T(8,128)(2,1)S(1)} %get-tuple-element.38), channel_id=1, source_target_pairs={{0,4},{2,6},{4,8},{6,10},{8,12},{10,14},{12,16},{14,18},{16,20},{1... | collective-permute-start | bytes 786440 | tf_op jit(solution)/shard_map/cond/branch_0_fun/ppermute | solution.py:20
  13.6 1.8 %collective-permute-done.1 = bf16[2,128,512]{2,1,0:T(8,128)(2,1)S(1)} collective-permute-done((bf16[2,128,512]{2,1,0:T(8,128)(2,1)S(1)}, bf16[2,128,512]{2,1,0:T(8,128)(2,1)S(1)}, u32[]{:S(2)}, u32[]{:S(2)}) %collective-permute-start.1) | collective-permute-done | bytes 262176 | tf_op jit(solution)/shard_map/cond/branch_0_fun/ppermute | solution.py:40
  15.4 5.0 %collective-permute-done.2 = bf16[2,128,512]{2,1,0:T(8,128)(2,1)S(1)} collective-permute-done((bf16[2,128,512]{2,1,0:T(8,128)(2,1)S(1)}, bf16[2,128,512]{2,1,0:T(8,128)(2,1)S(1)}, u32[]{:S(2)}, u32[]{:S(2)}) %collective-permute-start.2) | collective-permute-done | bytes 262176 | tf_op jit(solution)/shard_map/cond/branch_0_fun/ppermute | solution.py:40
  20.5 1.3 %collective-permute-start.5 = (bf16[2,128,512]{2,1,0:T(8,128)(2,1)S(1)}, bf16[2,128,512]{2,1,0:T(8,128)(2,1)S(1)}, u32[]{:S(2)}, u32[]{:S(2)}) collective-permute-start(bf16[2,128,512]{2,1,0:T(8,128)(2,1)S(1)} %select_select_fusion), channel_id=1, source_target_pairs={{0,4},{8,12},{16,20},{24,28},{1,5},{9,13},{17,21},{25,29}} | collective-permute-start | bytes 786440 | tf_op jit(solution)/shard_map/cond/branch_0_fun/ppermute | solution.py:51
  21.9 3.7 %collective-permute-done.5 = bf16[2,128,512]{2,1,0:T(8,128)(2,1)S(1)} collective-permute-done((bf16[2,128,512]{2,1,0:T(8,128)(2,1)S(1)}, bf16[2,128,512]{2,1,0:T(8,128)(2,1)S(1)}, u32[]{:S(2)}, u32[]{:S(2)}) %collective-permute-start.5) | collective-permute-done | bytes 262176 | tf_op jit(solution)/shard_map/cond/branch_0_fun/ppermute | solution.py:51
  25.7 1.3 %collective-permute-start.6 = (bf16[2,128,512]{2,1,0:T(8,128)(2,1)S(1)}, bf16[2,128,512]{2,1,0:T(8,128)(2,1)S(1)}, u32[]{:S(2)}, u32[]{:S(2)}) collective-permute-start(bf16[2,128,512]{2,1,0:T(8,128)(2,1)S(1)} %broadcast_select_fusion), channel_id=1, source_target_pairs={{0,2},{4,6},{8,10},{12,14},{16,18},{20,22},{24,26},{28,30},{1,3},{... | collective-permute-start | bytes 786440 | tf_op jit(solution)/shard_map/cond/branch_0_fun/ppermute | solution.py:51
  27.0 1.1 %collective-permute-done.6 = bf16[2,128,512]{2,1,0:T(8,128)(2,1)S(1)} collective-permute-done((bf16[2,128,512]{2,1,0:T(8,128)(2,1)S(1)}, bf16[2,128,512]{2,1,0:T(8,128)(2,1)S(1)}, u32[]{:S(2)}, u32[]{:S(2)}) %collective-permute-start.6) | collective-permute-done | bytes 262176 | tf_op jit(solution)/shard_map/cond/branch_0_fun/ppermute | solution.py:51
  28.2 16.5 %tree_attention_6.1 = (bf16[256,4096]{1,0:T(8,128)(2,1)}, bf16[256,4096]{1,0:T(8,128)(2,1)}, f32[2,256,512]{2,1,0:T(8,128)S(1)}, f32[2,128,512]{2,1,0:T(8,128)S(...) custom-call(s32[32]{0:T(128)S(1)} %copy-done.2, ...), custom_call_target="tpu_custom_call" | custom-call | tf_op jit(solution)/shard_map/cond/branch_0_fun/tree_attention_6/pallas_call | solution.py:308
  44.6 0.7 copy-done
  45.3 2.3 %collective-permute-start.9 = (bf16[2,256,512]{2,1,0:T(8,128)(2,1)S(1)}, bf16[2,256,512]{2,1,0:T(8,128)(2,1)S(1)}, u32[]{:S(2)}, u32[]{:S(2)}) collective-permute-start(bf16[2,256,512]{2,1,0:T(8,128)(2,1)S(1)} %get-tuple-element.48), channel_id=1, source_target_pairs={{0,2},{2,0},{4,6},{6,4},{8,10},{10,8},{12,14},{14,12},{16,18},{18,... | collective-permute-start | bytes 1572872 | tf_op jit(solution)/shard_map/cond/branch_0_fun/ppermute | solution.py:384
  47.6 1.3 %collective-permute-start.8 = (bf16[2,128,512]{2,1,0:T(8,128)(2,1)S(1)}, bf16[2,128,512]{2,1,0:T(8,128)(2,1)S(1)}, u32[]{:S(2)}, u32[]{:S(2)}) collective-permute-start(bf16[2,128,512]{2,1,0:T(8,128)(2,1)S(1)} %convert_element_type.74), channel_id=1, source_target_pairs={{2,0},{6,4},{10,8},{14,12},{18,16},{22,20},{26,24},{30,28},{3,1},{... | collective-permute-start | bytes 786440 | tf_op jit(solution)/shard_map/cond/branch_0_fun/ppermute | solution.py:68
  49.5 1.5 %collective-permute-done.8 = bf16[2,128,512]{2,1,0:T(8,128)(2,1)S(1)} collective-permute-done((bf16[2,128,512]{2,1,0:T(8,128)(2,1)S(1)}, bf16[2,128,512]{2,1,0:T(8,128)(2,1)S(1)}, u32[]{:S(2)}, u32[]{:S(2)}) %collective-permute-start.8) | collective-permute-done | bytes 262176 | tf_op jit(solution)/shard_map/cond/branch_0_fun/ppermute | solution.py:68
  51.1 1.3 %collective-permute-start.12 = (bf16[2,128,512]{2,1,0:T(8,128)(2,1)S(1)}, bf16[2,128,512]{2,1,0:T(8,128)(2,1)S(1)}, u32[]{:S(2)}, u32[]{:S(2)}) collective-permute-start(bf16[2,128,512]{2,1,0:T(8,128)(2,1)S(1)} %fusion.6), channel_id=1, source_target_pairs={{4,0},{8,12},{16,20},{24,28},{5,1},{9,13},{17,21},{25,29}} | collective-permute-start | bytes 786440 | tf_op jit(solution)/shard_map/cond/branch_0_fun/ppermute | solution.py:68
  53.8 0.8 add_convert_fusion
  54.6 1.3 %collective-permute-start.10 = (bf16[2,128,512]{2,1,0:T(8,128)(2,1)}, bf16[2,128,512]{2,1,0:T(8,128)(2,1)}, u32[]{:S(2)}, u32[]{:S(2)}) collective-permute-start(bf16[2,128,512]{2,1,0:T(8,128)(2,1)} %add_convert_fusion), channel_id=1, source_target_pairs={{4,0},{6,2},{8,4},{10,6},{12,8},{14,10},{16,12},{18,14},{20,16},{2... | collective-permute-start | bytes 786440 | tf_op jit(solution)/shard_map/cond/branch_0_fun/ppermute | solution.py:20
  55.9 9.3 %collective-permute-done.12 = bf16[2,128,512]{2,1,0:T(8,128)(2,1)S(1)} collective-permute-done((bf16[2,128,512]{2,1,0:T(8,128)(2,1)S(1)}, bf16[2,128,512]{2,1,0:T(8,128)(2,1)S(1)}, u32[]{:S(2)}, u32[]{:S(2)}) %collective-permute-start.12) | collective-permute-done | bytes 262176 | tf_op jit(solution)/shard_map/cond/branch_0_fun/ppermute | solution.py:68
  65.2 0.8 fusion.7
  66.0 1.3 %collective-permute-start.15 = (bf16[2,128,512]{2,1,0:T(8,128)(2,1)}, bf16[2,128,512]{2,1,0:T(8,128)(2,1)S(1)}, u32[]{:S(2)}, u32[]{:S(2)}) collective-permute-start(bf16[2,128,512]{2,1,0:T(8,128)(2,1)} %fusion.7), channel_id=1, source_target_pairs={{28,0},{29,1}} | collective-permute-start | bytes 786440 | tf_op jit(solution)/shard_map/cond/branch_0_fun/ppermute | solution.py:68
  67.3 1.3 %collective-permute-start.14 = (bf16[2,128,512]{2,1,0:T(8,128)(2,1)}, bf16[2,128,512]{2,1,0:T(8,128)(2,1)S(1)}, u32[]{:S(2)}, u32[]{:S(2)}) collective-permute-start(bf16[2,128,512]{2,1,0:T(8,128)(2,1)} %fusion.7), channel_id=1, source_target_pairs={{20,0},{21,1}} | collective-permute-start | bytes 786440 | tf_op jit(solution)/shard_map/cond/branch_0_fun/ppermute | solution.py:68
  68.6 1.3 %collective-permute-start.13 = (bf16[2,128,512]{2,1,0:T(8,128)(2,1)}, bf16[2,128,512]{2,1,0:T(8,128)(2,1)}, u32[]{:S(2)}, u32[]{:S(2)}) collective-permute-start(bf16[2,128,512]{2,1,0:T(8,128)(2,1)} %fusion.7), channel_id=1, source_target_pairs={{12,0},{13,1}} | collective-permute-start | bytes 786440 | tf_op jit(solution)/shard_map/cond/branch_0_fun/ppermute | solution.py:68
  70.0 1.8 %collective-permute-done.10 = bf16[2,128,512]{2,1,0:T(8,128)(2,1)} collective-permute-done((bf16[2,128,512]{2,1,0:T(8,128)(2,1)}, bf16[2,128,512]{2,1,0:T(8,128)(2,1)}, u32[]{:S(2)}, u32[]{:S(2)}) %collective-permute-start.10) | collective-permute-done | bytes 262176 | tf_op jit(solution)/shard_map/cond/branch_0_fun/ppermute | solution.py:20
  71.8 1.1 %add_bitcast_fusion = (f32[128,512]{1,0:T(8,128)S(1)}, f32[128,512]{1,0:T(8,128)S(1)}) fusion(bf16[2,128,512]{2,1,0:T(8,128)(2,1)S(1)} %collective-permute-done.11, bf16[2,128,512]{2,1,0:T(8,128)(2,1)} %collective-permute-done.10, bf16[2,256,512]{2,1,0:T(8,128)(2,1)S(1)} %collective-permute-done.9, pred[]{:T(512)S(6)} %eq.71), kind=kLoop, calls=%fused_computation.18 | loop fusion | flops 786432 | bytes 1310721 | tf_op jit(solution)/shard_map/cond/branch_0_fun/jit(_where)/broadcast_in_dim | solution.py:399
  72.9 4.7 %collective-permute-done.15 = bf16[2,128,512]{2,1,0:T(8,128)(2,1)S(1)} collective-permute-done((bf16[2,128,512]{2,1,0:T(8,128)(2,1)}, bf16[2,128,512]{2,1,0:T(8,128)(2,1)S(1)}, u32[]{:S(2)}, u32[]{:S(2)}) %collective-permute-start.15) | collective-permute-done | bytes 262176 | tf_op jit(solution)/shard_map/cond/branch_0_fun/ppermute | solution.py:68
  77.6 2.7 %collective-permute-done.14 = bf16[2,128,512]{2,1,0:T(8,128)(2,1)S(1)} collective-permute-done((bf16[2,128,512]{2,1,0:T(8,128)(2,1)}, bf16[2,128,512]{2,1,0:T(8,128)(2,1)S(1)}, u32[]{:S(2)}, u32[]{:S(2)}) %collective-permute-start.14) | collective-permute-done | bytes 262176 | tf_op jit(solution)/shard_map/cond/branch_0_fun/ppermute | solution.py:68
  80.3 2.8 %collective-permute-done.13 = bf16[2,128,512]{2,1,0:T(8,128)(2,1)} collective-permute-done((bf16[2,128,512]{2,1,0:T(8,128)(2,1)}, bf16[2,128,512]{2,1,0:T(8,128)(2,1)}, u32[]{:S(2)}, u32[]{:S(2)}) %collective-permute-start.13) | collective-permute-done | bytes 262176 | tf_op jit(solution)/shard_map/cond/branch_0_fun/ppermute | solution.py:68
  83.1 1.1 %convert_add_fusion = f32[2,128,512]{2,1,0:T(8,128)S(1)} fusion(bf16[2,128,512]{2,1,0:T(8,128)(2,1)S(1)} %collective-permute-done.15, bf16[2,128,512]{2,1,0:T(8,128)(2,1)S(1)} %collective-permute-done.14, bf16[2,128,512]{2,1,0:T(8,128)(2,1)} %collective-permute-done.13, bf16[2,128,512]{2,1,0:T(8,128)(2,1)S(1)} %collective-permute-done.12, ...), kind=kLoop, calls=%fused_computation.11 | loop fusion | flops 1310720 | bytes 2359296 | tf_op jit(solution)/shard_map/cond/branch_0_fun/add | solution.py:72
  84.3 1.1 %fusion.1 = (bf16[256,512]{1,0:T(8,128)(2,1)}, bf16[256,512]{1,0:T(8,128)(2,1)}) fusion(f32[2,256,512]{2,1,0:T(8,128)S(1)} %get-tuple-element.44, f32[128,512]{1,0:T(8,128)S(1)} %get-tuple-element.87, f32[128,512]{1,0:T(8,128)S(1)} %get-tuple-element.85, pred[256]{0:T(512)(128)(4,1)S(1)} %get-tuple-element.89, pred[256]{0:T(512)(128)(4,1)S(1)} %get-tuple-element.90, ...), kind=kLoop, calls=%fused_computation.3 | loop fusion | flops 1310720 | bytes 2621952 | tf_op jit(solution)/shard_map/cond/branch_0_fun/convert_element_type | solution.py:401
  (23 shorter events, 3.0 us)
Async XLA Ops:
  3.1 25.0 %copy-start.2 = (s32[32]{0:T(128)S(1)}, s32[32]{0:T(128)}, u32[]{:S(2)}) copy-start(s32[32]{0:T(128)} %get-tuple-element.28.parents_ref) | copy-start | bytes 388 | tf_op jit(solution)/shard_map/cond
  3.1 10.4 %collective-permute-start = (bf16[2,128,512]{2,1,0:T(8,128)(2,1)S(1)}, bf16[2,128,512]{2,1,0:T(8,128)(2,1)S(1)}, u32[]{:S(2)}, u32[]{:S(2)}) collective-permute-start(bf16[2,128,512]{2,1,0:T(8,128)(2,1)S(1)} %get-tuple-element.37), channel_id=1, source_target_pairs={{0,8},{1,9}} | collective-permute-start | bytes 786440 | tf_op jit(solution)/shard_map/cond/branch_0_fun/ppermute | solution.py:40
  8.1 7.3 %collective-permute-start.1 = (bf16[2,128,512]{2,1,0:T(8,128)(2,1)S(1)}, bf16[2,128,512]{2,1,0:T(8,128)(2,1)S(1)}, u32[]{:S(2)}, u32[]{:S(2)}) collective-permute-start(bf16[2,128,512]{2,1,0:T(8,128)(2,1)S(1)} %get-tuple-element.37), channel_id=1, source_target_pairs={{0,16},{1,17}} | collective-permute-start | bytes 786440 | tf_op jit(solution)/shard_map/cond/branch_0_fun/ppermute | solution.py:40
  9.8 10.6 %collective-permute-start.2 = (bf16[2,128,512]{2,1,0:T(8,128)(2,1)S(1)}, bf16[2,128,512]{2,1,0:T(8,128)(2,1)S(1)}, u32[]{:S(2)}, u32[]{:S(2)}) collective-permute-start(bf16[2,128,512]{2,1,0:T(8,128)(2,1)S(1)} %get-tuple-element.37), channel_id=1, source_target_pairs={{0,24},{1,25}} | collective-permute-start | bytes 786440 | tf_op jit(solution)/shard_map/cond/branch_0_fun/ppermute | solution.py:40
  11.5 8.9 %collective-permute-start.3 = (bf16[2,128,512]{2,1,0:T(8,128)(2,1)S(1)}, bf16[2,128,512]{2,1,0:T(8,128)(2,1)S(1)}, u32[]{:S(2)}, u32[]{:S(2)}) collective-permute-start(bf16[2,128,512]{2,1,0:T(8,128)(2,1)S(1)} %get-tuple-element.38), channel_id=1, source_target_pairs={{0,4},{2,6},{4,8},{6,10},{8,12},{10,14},{12,16},{14,18},{16,20},{1... | collective-permute-start | bytes 786440 | tf_op jit(solution)/shard_map/cond/branch_0_fun/ppermute | solution.py:20
  12.8 7.6 %collective-permute-start.4 = (bf16[2,128,512]{2,1,0:T(8,128)(2,1)S(1)}, bf16[2,128,512]{2,1,0:T(8,128)(2,1)S(1)}, u32[]{:S(2)}, u32[]{:S(2)}) collective-permute-start(bf16[2,128,512]{2,1,0:T(8,128)(2,1)S(1)} %get-tuple-element.38), channel_id=1, source_target_pairs={{2,8},{6,12},{10,16},{14,20},{18,24},{22,28},{3,9},{7,13},{11,17},... | collective-permute-start | bytes 786440 | tf_op jit(solution)/shard_map/cond/branch_0_fun/ppermute | solution.py:371
  20.5 5.2 %collective-permute-start.5 = (bf16[2,128,512]{2,1,0:T(8,128)(2,1)S(1)}, bf16[2,128,512]{2,1,0:T(8,128)(2,1)S(1)}, u32[]{:S(2)}, u32[]{:S(2)}) collective-permute-start(bf16[2,128,512]{2,1,0:T(8,128)(2,1)S(1)} %select_select_fusion), channel_id=1, source_target_pairs={{0,4},{8,12},{16,20},{24,28},{1,5},{9,13},{17,21},{25,29}} | collective-permute-start | bytes 786440 | tf_op jit(solution)/shard_map/cond/branch_0_fun/ppermute | solution.py:51
  21.8 6.3 %collective-permute-start.7 = (bf16[2,256,512]{2,1,0:T(8,128)(2,1)S(1)}, bf16[2,256,512]{2,1,0:T(8,128)(2,1)S(1)}, u32[]{:S(2)}, u32[]{:S(2)}) collective-permute-start(bf16[2,256,512]{2,1,0:T(8,128)(2,1)S(1)} %pad_maximum_fusion), channel_id=1, source_target_pairs={{0,2},{2,0},{4,6},{6,4},{8,10},{10,8},{12,14},{14,12},{16,18},{18,... | collective-permute-start | bytes 1572872 | tf_op jit(solution)/shard_map/cond/branch_0_fun/ppermute | solution.py:373
  25.7 2.4 %collective-permute-start.6 = (bf16[2,128,512]{2,1,0:T(8,128)(2,1)S(1)}, bf16[2,128,512]{2,1,0:T(8,128)(2,1)S(1)}, u32[]{:S(2)}, u32[]{:S(2)}) collective-permute-start(bf16[2,128,512]{2,1,0:T(8,128)(2,1)S(1)} %broadcast_select_fusion), channel_id=1, source_target_pairs={{0,2},{4,6},{8,10},{12,14},{16,18},{20,22},{24,26},{28,30},{1,3},{... | collective-permute-start | bytes 786440 | tf_op jit(solution)/shard_map/cond/branch_0_fun/ppermute | solution.py:51
  44.6 0.7 copy-start
  45.3 5.7 %collective-permute-start.9 = (bf16[2,256,512]{2,1,0:T(8,128)(2,1)S(1)}, bf16[2,256,512]{2,1,0:T(8,128)(2,1)S(1)}, u32[]{:S(2)}, u32[]{:S(2)}) collective-permute-start(bf16[2,256,512]{2,1,0:T(8,128)(2,1)S(1)} %get-tuple-element.48), channel_id=1, source_target_pairs={{0,2},{2,0},{4,6},{6,4},{8,10},{10,8},{12,14},{14,12},{16,18},{18,... | collective-permute-start | bytes 1572872 | tf_op jit(solution)/shard_map/cond/branch_0_fun/ppermute | solution.py:384
  47.6 3.4 %collective-permute-start.8 = (bf16[2,128,512]{2,1,0:T(8,128)(2,1)S(1)}, bf16[2,128,512]{2,1,0:T(8,128)(2,1)S(1)}, u32[]{:S(2)}, u32[]{:S(2)}) collective-permute-start(bf16[2,128,512]{2,1,0:T(8,128)(2,1)S(1)} %convert_element_type.74), channel_id=1, source_target_pairs={{2,0},{6,4},{10,8},{14,12},{18,16},{22,20},{26,24},{30,28},{3,1},{... | collective-permute-start | bytes 786440 | tf_op jit(solution)/shard_map/cond/branch_0_fun/ppermute | solution.py:68
  51.1 14.1 %collective-permute-start.12 = (bf16[2,128,512]{2,1,0:T(8,128)(2,1)S(1)}, bf16[2,128,512]{2,1,0:T(8,128)(2,1)S(1)}, u32[]{:S(2)}, u32[]{:S(2)}) collective-permute-start(bf16[2,128,512]{2,1,0:T(8,128)(2,1)S(1)} %fusion.6), channel_id=1, source_target_pairs={{4,0},{8,12},{16,20},{24,28},{5,1},{9,13},{17,21},{25,29}} | collective-permute-start | bytes 786440 | tf_op jit(solution)/shard_map/cond/branch_0_fun/ppermute | solution.py:68
  53.1 16.9 %collective-permute-start.11 = (bf16[2,128,512]{2,1,0:T(8,128)(2,1)}, bf16[2,128,512]{2,1,0:T(8,128)(2,1)S(1)}, u32[]{:S(2)}, u32[]{:S(2)}) collective-permute-start(bf16[2,128,512]{2,1,0:T(8,128)(2,1)} %copy-done), channel_id=1, source_target_pairs={{8,2},{12,6},{16,10},{20,14},{24,18},{28,22},{9,3},{13,7},{17,11},... | collective-permute-start | bytes 786440 | tf_op jit(solution)/shard_map/cond/branch_0_fun/ppermute | solution.py:385
  54.6 17.2 %collective-permute-start.10 = (bf16[2,128,512]{2,1,0:T(8,128)(2,1)}, bf16[2,128,512]{2,1,0:T(8,128)(2,1)}, u32[]{:S(2)}, u32[]{:S(2)}) collective-permute-start(bf16[2,128,512]{2,1,0:T(8,128)(2,1)} %add_convert_fusion), channel_id=1, source_target_pairs={{4,0},{6,2},{8,4},{10,6},{12,8},{14,10},{16,12},{18,14},{20,16},{2... | collective-permute-start | bytes 786440 | tf_op jit(solution)/shard_map/cond/branch_0_fun/ppermute | solution.py:20
  66.0 11.6 %collective-permute-start.15 = (bf16[2,128,512]{2,1,0:T(8,128)(2,1)}, bf16[2,128,512]{2,1,0:T(8,128)(2,1)S(1)}, u32[]{:S(2)}, u32[]{:S(2)}) collective-permute-start(bf16[2,128,512]{2,1,0:T(8,128)(2,1)} %fusion.7), channel_id=1, source_target_pairs={{28,0},{29,1}} | collective-permute-start | bytes 786440 | tf_op jit(solution)/shard_map/cond/branch_0_fun/ppermute | solution.py:68
  67.3 13.0 %collective-permute-start.14 = (bf16[2,128,512]{2,1,0:T(8,128)(2,1)}, bf16[2,128,512]{2,1,0:T(8,128)(2,1)S(1)}, u32[]{:S(2)}, u32[]{:S(2)}) collective-permute-start(bf16[2,128,512]{2,1,0:T(8,128)(2,1)} %fusion.7), channel_id=1, source_target_pairs={{20,0},{21,1}} | collective-permute-start | bytes 786440 | tf_op jit(solution)/shard_map/cond/branch_0_fun/ppermute | solution.py:68
  68.6 14.5 %collective-permute-start.13 = (bf16[2,128,512]{2,1,0:T(8,128)(2,1)}, bf16[2,128,512]{2,1,0:T(8,128)(2,1)}, u32[]{:S(2)}, u32[]{:S(2)}) collective-permute-start(bf16[2,128,512]{2,1,0:T(8,128)(2,1)} %fusion.7), channel_id=1, source_target_pairs={{12,0},{13,1}} | collective-permute-start | bytes 786440 | tf_op jit(solution)/shard_map/cond/branch_0_fun/ppermute | solution.py:68

commit v2 on v1

--- a/solution.py
+++ b/solution.py
@@ -12,6 +12,9 @@
 BLOCK_TOKENS = 128
 HOPS = 3
 LAYER = 4
+SUB_HEADS = 2
+SPAN = 2
+QUICK = (2, 3, 4, 5)
 
 
 def passed_along(array, by):
@@ -66,7 +69,7 @@
     for at, stage in enumerate(stages):
         sent = total.astype(jnp.bfloat16)
         arrived = [lax.ppermute(sent, "ctx", pairs) for pairs in stage]
-        if at == 0:
+        if at == 1:
             arrived[0], *after = lax.optimization_barrier((arrived[0], *after))
         for piece in arrived:
             total = total + piece.astype(jnp.float32)
@@ -74,7 +77,8 @@
 
 
 def export_kernel(
-    blocks_here, parents_ref, k_ref, v_ref, choice_ref, crowded_ref, first_ref, sent_ref, reach_ref
+    blocks_here, parents_ref, k_ref, v_ref, choice_ref, crowded_ref, first_ref, sent_ref,
+    reach_ref, choices_ref
 ):
     block_count = parents_ref.shape[0]
     for b in range(block_count):
@@ -93,10 +97,11 @@
             read = last > device
             count = count + read.astype(jnp.int32)
             choice = jnp.where(read, slot, choice)
-        choice_ref[device] = choice
+        choices_ref[device] = choice
         crowded = jnp.maximum(crowded, count)
     crowded_ref[0] = crowded
-    mine = choice_ref[lax.axis_index("ctx")]
+    mine = choices_ref[lax.axis_index("ctx")]
+    choice_ref[0] = mine
     rows = pl.ds(pl.multiple_of(mine * BLOCK_TOKENS, BLOCK_TOKENS), BLOCK_TOKENS)
     for which, ref in enumerate((k_ref, v_ref)):
         first_ref[which] = ref[:BLOCK_TOKENS]
@@ -112,14 +117,17 @@
     return pl.pallas_call(
         functools.partial(export_kernel, blocks_here),
         out_shape=[
-            jax.ShapeDtypeStruct((block_count // blocks_here,), jnp.int32),
+            jax.ShapeDtypeStruct((1,), jnp.int32),
             jax.ShapeDtypeStruct((1,), jnp.int32),
             pair,
             pair,
         ],
         in_specs=[smem, vmem, vmem],
         out_specs=[smem, smem, vmem, vmem],
-        scratch_shapes=[pltpu.SMEM((block_count,), jnp.int32)],
+        scratch_shapes=[
+            pltpu.SMEM((block_count,), jnp.int32),
+            pltpu.SMEM((block_count // blocks_here,), jnp.int32),
+        ],
         name="exported",
     )(parents, key, value)
 
@@ -134,9 +142,9 @@
 
 
 def attention_kernel(
-    plan, blocks_here, heads_per_group, parents_ref, q_ref, do_ref, k_own, v_own, root_ref, *rest
+    plan, blocks_here, heads_per_group, span, parents_ref, q_ref, do_ref, k_own, v_own, root_ref, *rest
 ):
-    held_counts, slot_of, chunk_heads, sub_heads, skew = plan
+    held_counts, slot_of, quick_counts = plan
     arrivals = rest[: len(held_counts)]
     (out_ref, gq_ref, gown_ref, groot_ref) = rest[len(held_counts) : len(held_counts) + 4]
     departures = rest[len(held_counts) + 4 : 2 * len(held_counts) + 4]
@@ -144,7 +152,8 @@
     own_base = 1 + sum(held_counts)
     scale = 1.0 / math.sqrt(HEAD_WIDTH)
     log2e = math.log2(math.e)
-    rows = sub_heads * BLOCK_TOKENS
+    rows = SUB_HEADS * BLOCK_TOKENS
+    groups = [slice(g * HEAD_WIDTH, (g + 1) * HEAD_WIDTH) for g in range(span)]
     most_seen = slots.shape[1]
 
     @pl.when(pl.program_id(0) == 0)
@@ -179,47 +188,50 @@
 
             counts[qb] = jnp.where(own > 0, count + 1, 1)
 
-    k_all[0] = root_ref[0]
-    v_all[0] = root_ref[1]
-    at = 1
-    for arrival, count in zip(arrivals, held_counts):
-        for e in range(count):
-            part = slice(e * BLOCK_TOKENS, (e + 1) * BLOCK_TOKENS)
-            k_all[at] = arrival[0, part]
-            v_all[at] = arrival[1, part]
-            at += 1
-    for b in range(blocks_here):
-        k_all[own_base + b] = k_own[b * BLOCK_TOKENS : (b + 1) * BLOCK_TOKENS]
-        v_all[own_base + b] = v_own[b * BLOCK_TOKENS : (b + 1) * BLOCK_TOKENS]
+    for g, cols in enumerate(groups):
+        k_all[g, 0] = root_ref[0, :, cols]
+        v_all[g, 0] = root_ref[1, :, cols]
+        at = 1
+        for arrival, count in zip(arrivals, held_counts):
+            for e in range(count):
+                part = slice(e * BLOCK_TOKENS, (e + 1) * BLOCK_TOKENS)
+                k_all[g, at] = arrival[0, part, cols]
+                v_all[g, at] = arrival[1, part, cols]
+                at += 1
+        for b in range(blocks_here):
+            part = slice(b * BLOCK_TOKENS, (b + 1) * BLOCK_TOKENS)
+            k_all[g, own_base + b] = k_own[part, cols]
+            v_all[g, own_base + b] = v_own[part, cols]
     gk_acc[...] = jnp.zeros_like(gk_acc)
     gv_acc[...] = jnp.zeros_like(gv_acc)
 
     def run_block(qb, seen):
         held = [slots[qb, j] for j in range(seen)]
         tokens = pl.ds(pl.multiple_of(qb * BLOCK_TOKENS, BLOCK_TOKENS), BLOCK_TOKENS)
-
-        keys = jnp.concatenate([k_all[s] for s in held], axis=0)
-        values = jnp.concatenate([v_all[s] for s in held], axis=0)
+        quick = seen in quick_counts
+        chunk_heads = span * heads_per_group if quick else SUB_HEADS
+        skew = 1 if quick else 0
         split = lambda wide: [
             wide[:, j * BLOCK_TOKENS : (j + 1) * BLOCK_TOKENS] for j in range(seen)
         ]
 
-        def run_chunk(chunk, carry):
+        def run_chunk(chunk):
             def load(ref, sub):
                 return jnp.concatenate([ref[tokens, c] for c in columns(sub)], axis=0)
 
             def columns(sub):
-                return [
-                    pl.ds(
-                        pl.multiple_of((chunk * chunk_heads + sub * sub_heads + h) * HEAD_WIDTH, HEAD_WIDTH),
-                        HEAD_WIDTH,
-                    )
-                    for h in range(sub_heads)
-                ]
+                heads = [chunk * chunk_heads + sub * SUB_HEADS + h for h in range(SUB_HEADS)]
+                return [pl.ds(pl.multiple_of(h * HEAD_WIDTH, HEAD_WIDTH), HEAD_WIDTH) for h in heads]
+
+            def group_of(sub):
+                return (chunk * chunk_heads + sub * SUB_HEADS) // heads_per_group
+
+            def blocks(ref, sub):
+                return jnp.concatenate([ref[group_of(sub), s] for s in held], axis=0)
 
             def first(sub):
                 q, do = load(q_ref, sub), load(do_ref, sub)
-                return dot(q, keys, NT), dot(do, values, NT)
+                return dot(q, blocks(k_all, sub), NT), dot(do, blocks(v_all, sub), NT)
 
             def second(sub, scores, gprobs):
                 scores = split(scores)
@@ -233,7 +245,7 @@
                 inverse = 1.0 / total
                 probs = [r * inverse for r in raised]
                 weights = jnp.concatenate([p.astype(jnp.bfloat16) for p in probs], axis=1)
-                attended = dot(weights, values, NN).astype(jnp.bfloat16)
+                attended = dot(weights, blocks(v_all, sub), NN).astype(jnp.bfloat16)
                 for h, c in enumerate(columns(sub)):
                     out_ref[tokens, c] = attended[h * BLOCK_TOKENS : (h + 1) * BLOCK_TOKENS]
                 return probs, weights, attended, gprobs
@@ -247,16 +259,16 @@
                     [(p * (g - delta)).astype(jnp.bfloat16) for p, g in zip(probs, split(gprobs))],
                     axis=1,
                 )
-                grad_q = (dot(dscores, keys, NN) * scale).astype(jnp.bfloat16)
+                grad_q = (dot(dscores, blocks(k_all, sub), NN) * scale).astype(jnp.bfloat16)
                 for h, c in enumerate(columns(sub)):
                     gq_ref[tokens, c] = grad_q[h * BLOCK_TOKENS : (h + 1) * BLOCK_TOKENS]
                 gk = split(dot(q, dscores, TN))
                 gv = split(dot(do, weights, TN))
                 for s, x, y in zip(held, gk, gv):
-                    gk_acc[s] += x
-                    gv_acc[s] += y
-
-            subs = chunk_heads // sub_heads
+                    gk_acc[group_of(sub), s] += x
+                    gv_acc[group_of(sub), s] += y
+
+            subs = chunk_heads // SUB_HEADS
             one, two = {}, {}
             for turn in range(subs + 2 * skew):
                 if turn < subs:
@@ -265,9 +277,11 @@
                     two[turn - skew] = second(turn - skew, *one.pop(turn - skew))
                 if 0 <= turn - 2 * skew < subs:
                     third(turn - 2 * skew, *two.pop(turn - 2 * skew))
-            return carry
-
-        lax.fori_loop(0, heads_per_group // chunk_heads, run_chunk, 0)
+
+        if quick:
+            run_chunk(0)
+        else:
+            pl.loop(0, span * heads_per_group // SUB_HEADS)(run_chunk)
 
     @pl.loop(0, blocks_here)
     def _(qb):
@@ -275,21 +289,23 @@
         for seen in range(1, most_seen + 1):
             pl.when(seen_here == seen)(functools.partial(run_block, qb, seen))
 
-    def grads(slot):
-        return (gk_acc[slot] * scale).T, gv_acc[slot].T
-
-    for b in range(blocks_here):
-        part = slice(b * BLOCK_TOKENS, (b + 1) * BLOCK_TOKENS)
-        gown_ref[0, part], gown_ref[1, part] = grads(own_base + b)
-    groot_ref[0], groot_ref[1] = grads(0)
-    at = 1
-    for departure, count in zip(departures, held_counts):
-        for e in range(count):
-            part = slice(e * BLOCK_TOKENS, (e + 1) * BLOCK_TOKENS)
-            gk, gv = grads(at)
-            departure[0, part] = gk.astype(jnp.bfloat16)
-            departure[1, part] = gv.astype(jnp.bfloat16)
-            at += 1
+    for g, cols in enumerate(groups):
+
+        def grads(slot):
+            return (gk_acc[g, slot] * scale).T, gv_acc[g, slot].T
+
+        for b in range(blocks_here):
+            part = slice(b * BLOCK_TOKENS, (b + 1) * BLOCK_TOKENS)
+            gown_ref[0, part, cols], gown_ref[1, part, cols] = grads(own_base + b)
+        groot_ref[0, :, cols], groot_ref[1, :, cols] = grads(0)
+        at = 1
+        for departure, count in zip(departures, held_counts):
+            for e in range(count):
+                part = slice(e * BLOCK_TOKENS, (e + 1) * BLOCK_TOKENS)
+                gk, gv = grads(at)
+                departure[0, part, cols] = gk.astype(jnp.bfloat16)
+                departure[1, part, cols] = gv.astype(jnp.bfloat16)
+                at += 1
 
 
 def attention(plan, most_seen, parents, query, grad, key, value, root_pair, arrivals):
@@ -297,19 +313,21 @@
     blocks_here = tokens_here // BLOCK_TOKENS
     groups = key.shape[1] // HEAD_WIDTH
     heads_per_group = query.shape[1] // HEAD_WIDTH // groups
-    wide = pl.BlockSpec((tokens_here, heads_per_group * HEAD_WIDTH), lambda g, _: (0, g))
-    narrow = pl.BlockSpec((tokens_here, HEAD_WIDTH), lambda g, _: (0, g))
-    pair = lambda rows: pl.BlockSpec((2, rows, HEAD_WIDTH), lambda g, _: (0, 0, g))
+    span = SPAN if groups % SPAN == 0 else 1
+    width = span * HEAD_WIDTH
+    wide = pl.BlockSpec((tokens_here, heads_per_group * width), lambda g, _: (0, g))
+    narrow = pl.BlockSpec((tokens_here, width), lambda g, _: (0, g))
+    pair = lambda rows: pl.BlockSpec((2, rows, width), lambda g, _: (0, 0, g))
     arrival_specs = [pair(a.shape[1]) for a in arrivals]
     slot_count = 1 + sum(plan[0]) + blocks_here
     like = lambda array, kind: jax.ShapeDtypeStruct(array.shape, kind)
-    blocks = pltpu.VMEM((slot_count, BLOCK_TOKENS, HEAD_WIDTH), jnp.bfloat16)
-    sums = pltpu.VMEM((slot_count, HEAD_WIDTH, BLOCK_TOKENS), jnp.float32)
+    blocks = pltpu.VMEM((span, slot_count, BLOCK_TOKENS, HEAD_WIDTH), jnp.bfloat16)
+    sums = pltpu.VMEM((span, slot_count, HEAD_WIDTH, BLOCK_TOKENS), jnp.float32)
     return pl.pallas_call(
-        functools.partial(attention_kernel, plan, blocks_here, heads_per_group),
+        functools.partial(attention_kernel, plan, blocks_here, heads_per_group, span),
         grid_spec=pltpu.PrefetchScalarGridSpec(
             num_scalar_prefetch=1,
-            grid=(groups,),
+            grid=(groups // span,),
             in_specs=[wide, wide, narrow, narrow, pair(BLOCK_TOKENS)] + arrival_specs,
             out_specs=[wide, wide, pair(tokens_here), pair(BLOCK_TOKENS)] + arrival_specs,
             scratch_shapes=[
@@ -344,7 +362,7 @@
     (root_pair,) = spread_from_first(first)
     pieces = [passed_along(key_value, back) for back in range(HOPS, 0, -1)]
     slot_of = lambda position, back, slot: 1 + (HOPS - back) * blocks_here + slot
-    plan = ((blocks_here,) * HOPS, slot_of, 2, 2, 0)
+    plan = ((blocks_here,) * HOPS, slot_of, ())
     out, grad_q, own, root_terms, *terms = attention(
         plan, 1 + (HOPS + 1) * blocks_here, parents, query, output_cotangent, key, value,
         root_pair, pieces,
@@ -366,7 +384,7 @@
     odd = position % 2
     swap = [(i, i ^ 1) for i in range(devices)]
     skip = [(i, i + 3) for i in range(1, devices - 3, 2)]
-    mine = choice[position]
+    mine = choice[0]
     two_back = passed_along(sent, 2)
     three_back = lax.ppermute(sent, "ctx", skip)
     root_pair, two_back, three_back = spread_from_first(first, (two_back, three_back))
@@ -376,7 +394,7 @@
         odd = lax.rem(position, 2)
         return jnp.where(back == 2, 2, jnp.where(back == 1, 3 + odd, 1 + 2 * odd))
 
-    plan = ((1, 1, 2), slot_of, 8, 2, 1)
+    plan = ((1, 1, 2), slot_of, QUICK)
     out, grad_q, own, root_terms, g_three, g_two, g_across = attention(
         plan, 1 + HOPS + blocks_here, parents, query, output_cotangent, key, value, root_pair,
         [three_back, two_back, across],
@@ -387,17 +405,15 @@
     merged = wide32(g_two) + wide32(from_core[:, :BLOCK_TOKENS])
     from_two = passed_along(merged.astype(jnp.bfloat16), -2)
 
-    block = lax.broadcasted_iota(jnp.int32, (blocks_here, BLOCK_TOKENS, key.shape[1]), 0)
-    at_first = (block == 0) & (position == 0)
+    block = jnp.arange(blocks_here, dtype=jnp.int32)[:, None, None]
+    exported = (block == mine).astype(jnp.float32)
+    at_first = ((block == 0) & (position == 0)).astype(jnp.float32)
 
     def final(which):
-        returned = (
-            wide32(from_two[which]) + wide32(from_three[which])
-            + jnp.where(odd == 0, wide32(from_core[which, BLOCK_TOKENS:]), 0.0)
-        )
-        total = own[which].reshape(block.shape)
-        total = total + jnp.where(block == mine, returned[None], 0.0)
-        total = total + jnp.where(at_first, root_sum[which][None], 0.0)
+        returned = wide32(from_two[which]) + wide32(from_three[which])
+        returned = returned + jnp.where(odd == 0, wide32(from_core[which, BLOCK_TOKENS:]), 0.0)
+        total = own[which].reshape((blocks_here, BLOCK_TOKENS, key.shape[1]))
+        total = total + exported * returned[None] + at_first * root_sum[which][None]
         return total.astype(jnp.bfloat16).reshape(key.shape)
 
     return out, grad_q, final(0), final(1)

time: 85.9 us -> 83.9 us (0.977)
  Pallas kernels: 18.3 us -> 23.1 us
  waiting for transfers between devices: 34.6 us -> 30.3 us
  local copies, waits for them, and re-layouts: 1.4 us -> 0.12 us
  starting transfers between devices: 23.7 us -> 22.6 us
    pallas_call x1, Pallas kernels: 16.5 us -> 21.3 us  [attention(): pl.pallas_call(functools.partial(attention_kernel, plan, blocks_here, hea...]
    ppermute x5, waiting for transfers between devices: 21.1 us -> 17.2 us  [sum_to_first(): arrived = [lax.ppermute(sent, 'ctx', pairs) for pairs in stage]]
    mul x0 -> x1, other arithmetic: none -> 1.07 us  [final(): total = total + exported * returned[None] + at_first * root_sum[which][None]]
    broadcast_in_dim x1 -> x0, other arithmetic: 1.07 us -> none  [final(): total = total + jnp.where(block == mine, returned[None], 0.0)]
    ppermute x1, starting transfers between devices: 2.27 us -> 1.2 us  [run_one_block(): from_core = lax.ppermute(g_across, 'ctx', swap)]
  transfers between devices with their start and end apart: 16 -> 16, of which waited for: 10 -> 10; matrix products, arithmetic and copies ran while one was open for 5% -> 4% of each run, Pallas kernels for 0% -> 0%
where the time goes in v2:
time: 83.9 us; the launch traced here: 83 us
  waiting for transfers between devices  30.3 us (36%)
  Pallas kernels  23.1 us (28%)
  starting transfers between devices  22.6 us (27%)
  other arithmetic  5.3 us (6%)
  between operations  1.29 us (2%)
    pallas_call x1, Pallas kernels, attention(): pl.pallas_call(functools.partial(attention_kernel, plan, blocks_here, hea...  21.3 us
    ppermute x5, waiting for transfers between devices, sum_to_first(): arrived = [lax.ppermute(sent, 'ctx', pairs) for pairs in stage]  17.2 us
    ppermute x3, starting transfers between devices, spread_from_first(): lax.ppermute(held, 'ctx', [(b * LAYER, (b + j * stride) * LAYER) for b in...  8.32 us
    ppermute x3, waiting for transfers between devices, spread_from_first(): lax.ppermute(held, 'ctx', [(b * LAYER, (b + j * stride) * LAYER) for b in...  6.83 us
    ppermute x5, starting transfers between devices, sum_to_first(): arrived = [lax.ppermute(sent, 'ctx', pairs) for pairs in stage]  6.46 us
    ppermute x2, waiting for transfers between devices, spread_from_first(): held = jnp.where(here, lax.ppermute(held, 'ctx', pairs), held)  4.84 us
    ppermute x2, starting transfers between devices, spread_from_first(): held = jnp.where(here, lax.ppermute(held, 'ctx', pairs), held)  2.61 us
    ppermute x2, starting transfers between devices, passed_along(): return lax.ppermute(array, 'ctx', pairs)  2.6 us
  transfers between devices with their start and end apart: 16, of which 10 were waited for; matrix products, arithmetic and copies ran while one was open for 4% of the time, Pallas kernels for 0%

profile of v2, /device:TPU:0, one launch (start us, length us, event | category | flops | bytes accessed | tf_op | source)
XLA Modules:
  0.0 83.0 jit_solution(16067063940530720009)
XLA Ops:
  0.6 1.8 %exported.1 = (s32[1]{0:T(128)}, s32[1]{0:T(128)}, bf16[2,128,512]{2,1,0:T(8,128)(2,1)S(1)}, bf16[2,128,512]{2,1,0:T(8,128)(2,1)S(1)}) custom-call(s32[32]{0:T(128)} %parents_ref.1, bf16[256,512]{1,0:T(8,128)(2,1)} %k_ref.1, bf16[256,512]{1,0:T(8,128)(2,1)} %v_ref.1), custom_call_target="tpu_custom_call" | custom-call | tf_op jit(solution)/shard_map/exported/pallas_call | solution.py:117
  3.1 80.0 %conditional.1 = (bf16[256,4096]{1,0:T(8,128)(2,1)}, bf16[256,4096]{1,0:T(8,128)(2,1)}, bf16[256,512]{1,0:T(8,128)(2,1)}, bf16[256,512]{1,0:T(8,128)(2,1)}) conditional(s32[]{:T(128)} %bitcast.17, (bf16[2,128,512]{2,1,0:T(8,128)(2,1)S(1)}, bf16[2,128,512]{2,1,0:T(8,128)(2,1)S(1)}, s32[32]{0:T(128)}, bf16[256,4096]{1,0:T(8,128)(2,1)}, ...), branch_computations={%region_0.1_spmd, %region_1.2_spmd} | conditional | flops 6815806 | bytes 39061180 | solution.py:424
  3.1 4.9 %collective-permute-start = (bf16[2,128,512]{2,1,0:T(8,128)(2,1)S(1)}, bf16[2,128,512]{2,1,0:T(8,128)(2,1)S(1)}, u32[]{:S(2)}, u32[]{:S(2)}) collective-permute-start(bf16[2,128,512]{2,1,0:T(8,128)(2,1)S(1)} %get-tuple-element.37), channel_id=1, source_target_pairs={{0,8},{1,9}} | collective-permute-start | bytes 786440 | tf_op jit(solution)/shard_map/cond/branch_0_fun/ppermute | solution.py:43
  8.0 1.7 %collective-permute-start.1 = (bf16[2,128,512]{2,1,0:T(8,128)(2,1)S(1)}, bf16[2,128,512]{2,1,0:T(8,128)(2,1)S(1)}, u32[]{:S(2)}, u32[]{:S(2)}) collective-permute-start(bf16[2,128,512]{2,1,0:T(8,128)(2,1)S(1)} %get-tuple-element.37), channel_id=1, source_target_pairs={{0,16},{1,17}} | collective-permute-start | bytes 786440 | tf_op jit(solution)/shard_map/cond/branch_0_fun/ppermute | solution.py:43
  9.7 1.7 %collective-permute-start.2 = (bf16[2,128,512]{2,1,0:T(8,128)(2,1)S(1)}, bf16[2,128,512]{2,1,0:T(8,128)(2,1)S(1)}, u32[]{:S(2)}, u32[]{:S(2)}) collective-permute-start(bf16[2,128,512]{2,1,0:T(8,128)(2,1)S(1)} %get-tuple-element.37), channel_id=1, source_target_pairs={{0,24},{1,25}} | collective-permute-start | bytes 786440 | tf_op jit(solution)/shard_map/cond/branch_0_fun/ppermute | solution.py:43
  11.4 1.3 %collective-permute-start.3 = (bf16[2,128,512]{2,1,0:T(8,128)(2,1)S(1)}, bf16[2,128,512]{2,1,0:T(8,128)(2,1)S(1)}, u32[]{:S(2)}, u32[]{:S(2)}) collective-permute-start(bf16[2,128,512]{2,1,0:T(8,128)(2,1)S(1)} %get-tuple-element.38), channel_id=1, source_target_pairs={{0,4},{2,6},{4,8},{6,10},{8,12},{10,14},{12,16},{14,18},{16,20},{1... | collective-permute-start | bytes 786440 | tf_op jit(solution)/shard_map/cond/branch_0_fun/ppermute | solution.py:23
  12.7 0.7 collective-permute-start.4
  13.5 1.8 %collective-permute-done.1 = bf16[2,128,512]{2,1,0:T(8,128)(2,1)S(1)} collective-permute-done((bf16[2,128,512]{2,1,0:T(8,128)(2,1)S(1)}, bf16[2,128,512]{2,1,0:T(8,128)(2,1)S(1)}, u32[]{:S(2)}, u32[]{:S(2)}) %collective-permute-start.1) | collective-permute-done | bytes 262176 | tf_op jit(solution)/shard_map/cond/branch_0_fun/ppermute | solution.py:43
  15.3 5.0 %collective-permute-done.2 = bf16[2,128,512]{2,1,0:T(8,128)(2,1)S(1)} collective-permute-done((bf16[2,128,512]{2,1,0:T(8,128)(2,1)S(1)}, bf16[2,128,512]{2,1,0:T(8,128)(2,1)S(1)}, u32[]{:S(2)}, u32[]{:S(2)}) %collective-permute-start.2) | collective-permute-done | bytes 262176 | tf_op jit(solution)/shard_map/cond/branch_0_fun/ppermute | solution.py:43
  20.4 1.3 %collective-permute-start.5 = (bf16[2,128,512]{2,1,0:T(8,128)(2,1)S(1)}, bf16[2,128,512]{2,1,0:T(8,128)(2,1)S(1)}, u32[]{:S(2)}, u32[]{:S(2)}) collective-permute-start(bf16[2,128,512]{2,1,0:T(8,128)(2,1)S(1)} %select_select_fusion), channel_id=1, source_target_pairs={{0,4},{8,12},{16,20},{24,28},{1,5},{9,13},{17,21},{25,29}} | collective-permute-start | bytes 786440 | tf_op jit(solution)/shard_map/cond/branch_0_fun/ppermute | solution.py:54
  21.8 3.7 %collective-permute-done.5 = bf16[2,128,512]{2,1,0:T(8,128)(2,1)S(1)} collective-permute-done((bf16[2,128,512]{2,1,0:T(8,128)(2,1)S(1)}, bf16[2,128,512]{2,1,0:T(8,128)(2,1)S(1)}, u32[]{:S(2)}, u32[]{:S(2)}) %collective-permute-start.5) | collective-permute-done | bytes 262176 | tf_op jit(solution)/shard_map/cond/branch_0_fun/ppermute | solution.py:54
  25.6 1.3 %collective-permute-start.6 = (bf16[2,128,512]{2,1,0:T(8,128)(2,1)S(1)}, bf16[2,128,512]{2,1,0:T(8,128)(2,1)S(1)}, u32[]{:S(2)}, u32[]{:S(2)}) collective-permute-start(bf16[2,128,512]{2,1,0:T(8,128)(2,1)S(1)} %broadcast_select_fusion), channel_id=1, source_target_pairs={{0,2},{4,6},{8,10},{12,14},{16,18},{20,22},{24,26},{28,30},{1,3},{... | collective-permute-start | bytes 786440 | tf_op jit(solution)/shard_map/cond/branch_0_fun/ppermute | solution.py:54
  26.9 1.1 %collective-permute-done.6 = bf16[2,128,512]{2,1,0:T(8,128)(2,1)S(1)} collective-permute-done((bf16[2,128,512]{2,1,0:T(8,128)(2,1)S(1)}, bf16[2,128,512]{2,1,0:T(8,128)(2,1)S(1)}, u32[]{:S(2)}, u32[]{:S(2)}) %collective-permute-start.6) | collective-permute-done | bytes 262176 | tf_op jit(solution)/shard_map/cond/branch_0_fun/ppermute | solution.py:54
  28.1 21.3 %tree_attention_6.1 = (bf16[256,4096]{1,0:T(8,128)(2,1)}, bf16[256,4096]{1,0:T(8,128)(2,1)}, f32[2,256,512]{2,1,0:T(8,128)S(1)}, f32[2,128,512]{2,1,0:T(8,128)S(...) custom-call(s32[32]{0:T(128)S(1)} %copy-done.3, ...), custom_call_target="tpu_custom_call" | custom-call | tf_op jit(solution)/shard_map/cond/branch_0_fun/tree_attention_6/pallas_call | solution.py:326
  49.4 1.3 %collective-permute-start.8 = (bf16[2,128,512]{2,1,0:T(8,128)(2,1)S(1)}, bf16[2,128,512]{2,1,0:T(8,128)(2,1)S(1)}, u32[]{:S(2)}, u32[]{:S(2)}) collective-permute-start(bf16[2,128,512]{2,1,0:T(8,128)(2,1)S(1)} %convert_element_type.89), channel_id=1, source_target_pairs={{2,0},{6,4},{10,8},{14,12},{18,16},{22,20},{26,24},{30,28},{3,1},{... | collective-permute-start | bytes 786440 | tf_op jit(solution)/shard_map/cond/branch_0_fun/ppermute | solution.py:71
  50.7 1.2 %collective-permute-start.10 = (bf16[2,256,512]{2,1,0:T(8,128)(2,1)S(1)}, bf16[2,256,512]{2,1,0:T(8,128)(2,1)}, u32[]{:S(2)}, u32[]{:S(2)}) collective-permute-start(bf16[2,256,512]{2,1,0:T(8,128)(2,1)S(1)} %get-tuple-element.48), channel_id=1, source_target_pairs={{0,2},{2,0},{4,6},{6,4},{8,10},{10,8},{12,14},{14,12},{16,18},{18,... | collective-permute-start | bytes 1572872 | tf_op jit(solution)/shard_map/cond/branch_0_fun/ppermute | solution.py:402
  52.0 0.9 %collective-permute-done.8 = bf16[2,128,512]{2,1,0:T(8,128)(2,1)S(1)} collective-permute-done((bf16[2,128,512]{2,1,0:T(8,128)(2,1)S(1)}, bf16[2,128,512]{2,1,0:T(8,128)(2,1)S(1)}, u32[]{:S(2)}, u32[]{:S(2)}) %collective-permute-start.8) | collective-permute-done | bytes 262176 | tf_op jit(solution)/shard_map/cond/branch_0_fun/ppermute | solution.py:71
  53.0 1.3 %collective-permute-start.9 = (bf16[2,128,512]{2,1,0:T(8,128)(2,1)S(1)}, bf16[2,128,512]{2,1,0:T(8,128)(2,1)S(1)}, u32[]{:S(2)}, u32[]{:S(2)}) collective-permute-start(bf16[2,128,512]{2,1,0:T(8,128)(2,1)S(1)} %fusion.6), channel_id=1, source_target_pairs={{4,0},{8,12},{16,20},{24,28},{5,1},{9,13},{17,21},{25,29}} | collective-permute-start | bytes 786440 | tf_op jit(solution)/shard_map/cond/branch_0_fun/ppermute | solution.py:71
  54.9 6.3 %collective-permute-done.9 = bf16[2,128,512]{2,1,0:T(8,128)(2,1)S(1)} collective-permute-done((bf16[2,128,512]{2,1,0:T(8,128)(2,1)S(1)}, bf16[2,128,512]{2,1,0:T(8,128)(2,1)S(1)}, u32[]{:S(2)}, u32[]{:S(2)}) %collective-permute-start.9) | collective-permute-done | bytes 262176 | tf_op jit(solution)/shard_map/cond/branch_0_fun/ppermute | solution.py:71
  61.3 1.3 %collective-permute-start.15 = (bf16[2,128,512]{2,1,0:T(8,128)(2,1)S(1)}, bf16[2,128,512]{2,1,0:T(8,128)(2,1)S(1)}, u32[]{:S(2)}, u32[]{:S(2)}) collective-permute-start(bf16[2,128,512]{2,1,0:T(8,128)(2,1)S(1)} %fusion.7), channel_id=1, source_target_pairs={{28,0},{29,1}} | collective-permute-start | bytes 786440 | tf_op jit(solution)/shard_map/cond/branch_0_fun/ppermute | solution.py:71
  62.6 1.3 %collective-permute-start.14 = (bf16[2,128,512]{2,1,0:T(8,128)(2,1)S(1)}, bf16[2,128,512]{2,1,0:T(8,128)(2,1)S(1)}, u32[]{:S(2)}, u32[]{:S(2)}) collective-permute-start(bf16[2,128,512]{2,1,0:T(8,128)(2,1)S(1)} %fusion.7), channel_id=1, source_target_pairs={{20,0},{21,1}} | collective-permute-start | bytes 786440 | tf_op jit(solution)/shard_map/cond/branch_0_fun/ppermute | solution.py:71
  63.9 1.3 %collective-permute-start.13 = (bf16[2,128,512]{2,1,0:T(8,128)(2,1)S(1)}, bf16[2,128,512]{2,1,0:T(8,128)(2,1)}, u32[]{:S(2)}, u32[]{:S(2)}) collective-permute-start(bf16[2,128,512]{2,1,0:T(8,128)(2,1)S(1)} %fusion.7), channel_id=1, source_target_pairs={{12,0},{13,1}} | collective-permute-start | bytes 786440 | tf_op jit(solution)/shard_map/cond/branch_0_fun/ppermute | solution.py:71
  65.3 0.7 collective-permute-start.12
  66.0 1.0 %add_convert_fusion = bf16[2,128,512]{2,1,0:T(8,128)(2,1)S(1)} fusion(bf16[2,128,512]{2,1,0:T(8,128)(2,1)S(1)} %get-tuple-element.46, bf16[2,256,512]{2,1,0:T(8,128)(2,1)} %collective-permute-done.10), kind=kLoop, calls=%fused_computation.13 | loop fusion | flops 524288 | bytes 786432 | tf_op jit(solution)/shard_map/cond/branch_0_fun/convert_element_type | solution.py:406
  67.0 1.3 %collective-permute-start.11 = (bf16[2,128,512]{2,1,0:T(8,128)(2,1)S(1)}, bf16[2,128,512]{2,1,0:T(8,128)(2,1)S(1)}, u32[]{:S(2)}, u32[]{:S(2)}) collective-permute-start(bf16[2,128,512]{2,1,0:T(8,128)(2,1)S(1)} %add_convert_fusion), channel_id=1, source_target_pairs={{4,0},{6,2},{8,4},{10,6},{12,8},{14,10},{16,12},{18,14},{20,16},{2... | collective-permute-start | bytes 786440 | tf_op jit(solution)/shard_map/cond/branch_0_fun/ppermute | solution.py:23
  68.3 4.3 %collective-permute-done.15 = bf16[2,128,512]{2,1,0:T(8,128)(2,1)S(1)} collective-permute-done((bf16[2,128,512]{2,1,0:T(8,128)(2,1)S(1)}, bf16[2,128,512]{2,1,0:T(8,128)(2,1)S(1)}, u32[]{:S(2)}, u32[]{:S(2)}) %collective-permute-start.15) | collective-permute-done | bytes 262176 | tf_op jit(solution)/shard_map/cond/branch_0_fun/ppermute | solution.py:71
  72.6 2.8 %collective-permute-done.14 = bf16[2,128,512]{2,1,0:T(8,128)(2,1)S(1)} collective-permute-done((bf16[2,128,512]{2,1,0:T(8,128)(2,1)S(1)}, bf16[2,128,512]{2,1,0:T(8,128)(2,1)S(1)}, u32[]{:S(2)}, u32[]{:S(2)}) %collective-permute-start.14) | collective-permute-done | bytes 262176 | tf_op jit(solution)/shard_map/cond/branch_0_fun/ppermute | solution.py:71
  75.4 2.8 %collective-permute-done.13 = bf16[2,128,512]{2,1,0:T(8,128)(2,1)} collective-permute-done((bf16[2,128,512]{2,1,0:T(8,128)(2,1)S(1)}, bf16[2,128,512]{2,1,0:T(8,128)(2,1)}, u32[]{:S(2)}, u32[]{:S(2)}) %collective-permute-start.13) | collective-permute-done | bytes 262176 | tf_op jit(solution)/shard_map/cond/branch_0_fun/ppermute | solution.py:71
  78.3 1.1 %convert_add_fusion = f32[2,128,512]{2,1,0:T(8,128)S(1)} fusion(bf16[2,128,512]{2,1,0:T(8,128)(2,1)S(1)} %collective-permute-done.15, bf16[2,128,512]{2,1,0:T(8,128)(2,1)S(1)} %collective-permute-done.14, bf16[2,128,512]{2,1,0:T(8,128)(2,1)} %collective-permute-done.13, bf16[2,128,512]{2,1,0:T(8,128)(2,1)S(1)} %collective-permute-done.9, ...), kind=kLoop, calls=%fused_computation.11 | loop fusion | flops 1310720 | bytes 2359296 | tf_op jit(solution)/shard_map/cond/branch_0_fun/add | solution.py:75
  79.5 1.4 %collective-permute-done.11 = bf16[2,128,512]{2,1,0:T(8,128)(2,1)S(1)} collective-permute-done((bf16[2,128,512]{2,1,0:T(8,128)(2,1)S(1)}, bf16[2,128,512]{2,1,0:T(8,128)(2,1)S(1)}, u32[]{:S(2)}, u32[]{:S(2)}) %collective-permute-start.11) | collective-permute-done | bytes 262176 | tf_op jit(solution)/shard_map/cond/branch_0_fun/ppermute | solution.py:23
  80.9 1.1 %add_bitcast_fusion = (f32[128,512]{1,0:T(8,128)S(1)}, f32[128,512]{1,0:T(8,128)S(1)}) fusion(bf16[2,128,512]{2,1,0:T(8,128)(2,1)S(1)} %collective-permute-done.12, bf16[2,128,512]{2,1,0:T(8,128)(2,1)S(1)} %collective-permute-done.11, bf16[2,256,512]{2,1,0:T(8,128)(2,1)} %collective-permute-done.10, pred[]{:T(512)S(6)} %eq.77), kind=kLoop, calls=%fused_computation.18 | loop fusion | flops 786432 | bytes 1310721 | tf_op jit(solution)/shard_map/cond/branch_0_fun/mul | solution.py:416
  81.9 1.1 %fusion.1 = (bf16[256,512]{1,0:T(8,128)(2,1)}, bf16[256,512]{1,0:T(8,128)(2,1)}) fusion(f32[2,256,512]{2,1,0:T(8,128)S(1)} %get-tuple-element.44, f32[128,512]{1,0:T(8,128)S(1)} %get-tuple-element.87, f32[128,512]{1,0:T(8,128)S(1)} %get-tuple-element.85, f32[256]{0:T(256)S(1)} %get-tuple-element.89, f32[256]{0:T(256)S(1)} %get-tuple-element.90, ...), kind=kLoop, calls=%fused_computation.3 | loop fusion | flops 1310720 | bytes 2623488 | tf_op jit(solution)/shard_map/cond/branch_0_fun/convert_element_type | solution.py:417
  (24 shorter events, 1.2 us)
Async XLA Ops:
  3.1 25.0 %copy-start.3 = (s32[32]{0:T(128)S(1)}, s32[32]{0:T(128)}, u32[]{:S(2)}) copy-start(s32[32]{0:T(128)} %get-tuple-element.28.parents_ref) | copy-start | bytes 388 | tf_op jit(solution)/shard_map/cond
  3.1 10.4 %collective-permute-start = (bf16[2,128,512]{2,1,0:T(8,128)(2,1)S(1)}, bf16[2,128,512]{2,1,0:T(8,128)(2,1)S(1)}, u32[]{:S(2)}, u32[]{:S(2)}) collective-permute-start(bf16[2,128,512]{2,1,0:T(8,128)(2,1)S(1)} %get-tuple-element.37), channel_id=1, source_target_pairs={{0,8},{1,9}} | collective-permute-start | bytes 786440 | tf_op jit(solution)/shard_map/cond/branch_0_fun/ppermute | solution.py:43
  8.0 7.3 %collective-permute-start.1 = (bf16[2,128,512]{2,1,0:T(8,128)(2,1)S(1)}, bf16[2,128,512]{2,1,0:T(8,128)(2,1)S(1)}, u32[]{:S(2)}, u32[]{:S(2)}) collective-permute-start(bf16[2,128,512]{2,1,0:T(8,128)(2,1)S(1)} %get-tuple-element.37), channel_id=1, source_target_pairs={{0,16},{1,17}} | collective-permute-start | bytes 786440 | tf_op jit(solution)/shard_map/cond/branch_0_fun/ppermute | solution.py:43
  9.7 10.6 %collective-permute-start.2 = (bf16[2,128,512]{2,1,0:T(8,128)(2,1)S(1)}, bf16[2,128,512]{2,1,0:T(8,128)(2,1)S(1)}, u32[]{:S(2)}, u32[]{:S(2)}) collective-permute-start(bf16[2,128,512]{2,1,0:T(8,128)(2,1)S(1)} %get-tuple-element.37), channel_id=1, source_target_pairs={{0,24},{1,25}} | collective-permute-start | bytes 786440 | tf_op jit(solution)/shard_map/cond/branch_0_fun/ppermute | solution.py:43
  11.4 8.9 %collective-permute-start.3 = (bf16[2,128,512]{2,1,0:T(8,128)(2,1)S(1)}, bf16[2,128,512]{2,1,0:T(8,128)(2,1)S(1)}, u32[]{:S(2)}, u32[]{:S(2)}) collective-permute-start(bf16[2,128,512]{2,1,0:T(8,128)(2,1)S(1)} %get-tuple-element.38), channel_id=1, source_target_pairs={{0,4},{2,6},{4,8},{6,10},{8,12},{10,14},{12,16},{14,18},{16,20},{1... | collective-permute-start | bytes 786440 | tf_op jit(solution)/shard_map/cond/branch_0_fun/ppermute | solution.py:23
  12.7 7.6 %collective-permute-start.4 = (bf16[2,128,512]{2,1,0:T(8,128)(2,1)S(1)}, bf16[2,128,512]{2,1,0:T(8,128)(2,1)S(1)}, u32[]{:S(2)}, u32[]{:S(2)}) collective-permute-start(bf16[2,128,512]{2,1,0:T(8,128)(2,1)S(1)} %get-tuple-element.38), channel_id=1, source_target_pairs={{2,8},{6,12},{10,16},{14,20},{18,24},{22,28},{3,9},{7,13},{11,17},... | collective-permute-start | bytes 786440 | tf_op jit(solution)/shard_map/cond/branch_0_fun/ppermute | solution.py:389
  20.4 5.2 %collective-permute-start.5 = (bf16[2,128,512]{2,1,0:T(8,128)(2,1)S(1)}, bf16[2,128,512]{2,1,0:T(8,128)(2,1)S(1)}, u32[]{:S(2)}, u32[]{:S(2)}) collective-permute-start(bf16[2,128,512]{2,1,0:T(8,128)(2,1)S(1)} %select_select_fusion), channel_id=1, source_target_pairs={{0,4},{8,12},{16,20},{24,28},{1,5},{9,13},{17,21},{25,29}} | collective-permute-start | bytes 786440 | tf_op jit(solution)/shard_map/cond/branch_0_fun/ppermute | solution.py:54
  21.8 6.3 %collective-permute-start.7 = (bf16[2,256,512]{2,1,0:T(8,128)(2,1)S(1)}, bf16[2,256,512]{2,1,0:T(8,128)(2,1)S(1)}, u32[]{:S(2)}, u32[]{:S(2)}) collective-permute-start(bf16[2,256,512]{2,1,0:T(8,128)(2,1)S(1)} %pad_maximum_fusion), channel_id=1, source_target_pairs={{0,2},{2,0},{4,6},{6,4},{8,10},{10,8},{12,14},{14,12},{16,18},{18,... | collective-permute-start | bytes 1572872 | tf_op jit(solution)/shard_map/cond/branch_0_fun/ppermute | solution.py:391
  25.6 2.4 %collective-permute-start.6 = (bf16[2,128,512]{2,1,0:T(8,128)(2,1)S(1)}, bf16[2,128,512]{2,1,0:T(8,128)(2,1)S(1)}, u32[]{:S(2)}, u32[]{:S(2)}) collective-permute-start(bf16[2,128,512]{2,1,0:T(8,128)(2,1)S(1)} %broadcast_select_fusion), channel_id=1, source_target_pairs={{0,2},{4,6},{8,10},{12,14},{16,18},{20,22},{24,26},{28,30},{1,3},{... | collective-permute-start | bytes 786440 | tf_op jit(solution)/shard_map/cond/branch_0_fun/ppermute | solution.py:54
  49.4 2.5 %copy-start = (bf16[2,128,512]{2,1,0:T(8,128)(2,1)}, bf16[2,128,512]{2,1,0:T(8,128)(2,1)S(1)}, u32[]{:S(2)}) copy-start(bf16[2,128,512]{2,1,0:T(8,128)(2,1)S(1)} %get-tuple-element.50) | copy-start | bytes 786436 | tf_op jit(solution)/shard_map/cond
  49.4 3.4 %collective-permute-start.8 = (bf16[2,128,512]{2,1,0:T(8,128)(2,1)S(1)}, bf16[2,128,512]{2,1,0:T(8,128)(2,1)S(1)}, u32[]{:S(2)}, u32[]{:S(2)}) collective-permute-start(bf16[2,128,512]{2,1,0:T(8,128)(2,1)S(1)} %convert_element_type.89), channel_id=1, source_target_pairs={{2,0},{6,4},{10,8},{14,12},{18,16},{22,20},{26,24},{30,28},{3,1},{... | collective-permute-start | bytes 786440 | tf_op jit(solution)/shard_map/cond/branch_0_fun/ppermute | solution.py:71
  50.7 10.5 %collective-permute-start.10 = (bf16[2,256,512]{2,1,0:T(8,128)(2,1)S(1)}, bf16[2,256,512]{2,1,0:T(8,128)(2,1)}, u32[]{:S(2)}, u32[]{:S(2)}) collective-permute-start(bf16[2,256,512]{2,1,0:T(8,128)(2,1)S(1)} %get-tuple-element.48), channel_id=1, source_target_pairs={{0,2},{2,0},{4,6},{6,4},{8,10},{10,8},{12,14},{14,12},{16,18},{18,... | collective-permute-start | bytes 1572872 | tf_op jit(solution)/shard_map/cond/branch_0_fun/ppermute | solution.py:402
  52.9 12.4 %copy-start.1 = (bf16[2,128,512]{2,1,0:T(8,128)(2,1)S(1)}, bf16[2,128,512]{2,1,0:T(8,128)(2,1)}, u32[]{:S(2)}) copy-start(bf16[2,128,512]{2,1,0:T(8,128)(2,1)} %copy-done) | copy-start | bytes 786436 | tf_op jit(solution)/shard_map/cond
  53.0 8.3 %collective-permute-start.9 = (bf16[2,128,512]{2,1,0:T(8,128)(2,1)S(1)}, bf16[2,128,512]{2,1,0:T(8,128)(2,1)S(1)}, u32[]{:S(2)}, u32[]{:S(2)}) collective-permute-start(bf16[2,128,512]{2,1,0:T(8,128)(2,1)S(1)} %fusion.6), channel_id=1, source_target_pairs={{4,0},{8,12},{16,20},{24,28},{5,1},{9,13},{17,21},{25,29}} | collective-permute-start | bytes 786440 | tf_op jit(solution)/shard_map/cond/branch_0_fun/ppermute | solution.py:71
  61.3 11.3 %collective-permute-start.15 = (bf16[2,128,512]{2,1,0:T(8,128)(2,1)S(1)}, bf16[2,128,512]{2,1,0:T(8,128)(2,1)S(1)}, u32[]{:S(2)}, u32[]{:S(2)}) collective-permute-start(bf16[2,128,512]{2,1,0:T(8,128)(2,1)S(1)} %fusion.7), channel_id=1, source_target_pairs={{28,0},{29,1}} | collective-permute-start | bytes 786440 | tf_op jit(solution)/shard_map/cond/branch_0_fun/ppermute | solution.py:71
  62.6 12.8 %collective-permute-start.14 = (bf16[2,128,512]{2,1,0:T(8,128)(2,1)S(1)}, bf16[2,128,512]{2,1,0:T(8,128)(2,1)S(1)}, u32[]{:S(2)}, u32[]{:S(2)}) collective-permute-start(bf16[2,128,512]{2,1,0:T(8,128)(2,1)S(1)} %fusion.7), channel_id=1, source_target_pairs={{20,0},{21,1}} | collective-permute-start | bytes 786440 | tf_op jit(solution)/shard_map/cond/branch_0_fun/ppermute | solution.py:71
  63.9 14.3 %collective-permute-start.13 = (bf16[2,128,512]{2,1,0:T(8,128)(2,1)S(1)}, bf16[2,128,512]{2,1,0:T(8,128)(2,1)}, u32[]{:S(2)}, u32[]{:S(2)}) collective-permute-start(bf16[2,128,512]{2,1,0:T(8,128)(2,1)S(1)} %fusion.7), channel_id=1, source_target_pairs={{12,0},{13,1}} | collective-permute-start | bytes 786440 | tf_op jit(solution)/shard_map/cond/branch_0_fun/ppermute | solution.py:71
  65.3 14.2 %collective-permute-start.12 = (bf16[2,128,512]{2,1,0:T(8,128)(2,1)S(1)}, bf16[2,128,512]{2,1,0:T(8,128)(2,1)S(1)}, u32[]{:S(2)}, u32[]{:S(2)}) collective-permute-start(bf16[2,128,512]{2,1,0:T(8,128)(2,1)S(1)} %copy-done.1), channel_id=1, source_target_pairs={{8,2},{12,6},{16,10},{20,14},{24,18},{28,22},{9,3},{13,7},{17,11},... | collective-permute-start | bytes 786440 | tf_op jit(solution)/shard_map/cond/branch_0_fun/ppermute | solution.py:403
  67.0 13.9 %collective-permute-start.11 = (bf16[2,128,512]{2,1,0:T(8,128)(2,1)S(1)}, bf16[2,128,512]{2,1,0:T(8,128)(2,1)S(1)}, u32[]{:S(2)}, u32[]{:S(2)}) collective-permute-start(bf16[2,128,512]{2,1,0:T(8,128)(2,1)S(1)} %add_convert_fusion), channel_id=1, source_target_pairs={{4,0},{6,2},{8,4},{10,6},{12,8},{14,10},{16,12},{18,14},{20,16},{2... | collective-permute-start | bytes 786440 | tf_op jit(solution)/shard_map/cond/branch_0_fun/ppermute | solution.py:23

commit v3 on v2

--- a/solution.py
+++ b/solution.py
@@ -47,8 +47,12 @@
         for j, piece in enumerate(arrived, 1):
             here = (position % LAYER == 0) & (layer % (stride * fan) == j * stride)
             held = jnp.where(here, piece, held)
-    held, *after = lax.optimization_barrier((held, *after))
+    after = list(after)
+    if after:
+        held, after[0] = lax.optimization_barrier((held, after[0]))
     for step in (2, 1):
+        if step == 1:
+            held, *after = lax.optimization_barrier((held, *after))
         pairs = [(i, i + step) for i in range(0, devices, 2 * step)]
         here = (position % (2 * step)) == step
         held = jnp.where(here, lax.ppermute(held, "ctx", pairs), held)

time: 83.9 us -> 85.6 us (1.020)
  starting transfers between devices: 22.6 us -> 27.3 us
  waiting for transfers between devices: 30.3 us -> 27.7 us
    ppermute x2, starting transfers between devices: 2.61 us -> 5.35 us  [spread_from_first(): held = jnp.where(here, lax.ppermute(held, 'ctx', pairs), held)]
    ppermute x3, waiting for transfers between devices: 6.83 us -> 4.71 us  [spread_from_first(): lax.ppermute(held, 'ctx', [(b * LAYER, (b + j * stride) * LAYER) for b in...]
    ppermute x1, starting transfers between devices: 0.07 us -> 2.03 us  [run_one_block(): lax.ppermute(jnp.concatenate([two_back, sent], axis=1), 'ctx', swap)]
where the time goes in v3:
time: 85.6 us; the launch traced here: 85.1 us
  waiting for transfers between devices  27.7 us (32%)
  starting transfers between devices  27.3 us (32%)
  Pallas kernels  23.1 us (27%)
  other arithmetic  5.31 us (6%)
  between operations  1.29 us (2%)
    pallas_call x1, Pallas kernels, attention(): pl.pallas_call(functools.partial(attention_kernel, plan, blocks_here, hea...  21.3 us
    ppermute x5, waiting for transfers between devices, sum_to_first(): arrived = [lax.ppermute(sent, 'ctx', pairs) for pairs in stage]  17.3 us
    ppermute x3, starting transfers between devices, spread_from_first(): lax.ppermute(held, 'ctx', [(b * LAYER, (b + j * stride) * LAYER) for b in...  8.32 us
    ppermute x5, starting transfers between devices, sum_to_first(): arrived = [lax.ppermute(sent, 'ctx', pairs) for pairs in stage]  6.46 us
    ppermute x2, starting transfers between devices, spread_from_first(): held = jnp.where(here, lax.ppermute(held, 'ctx', pairs), held)  5.35 us
    ppermute x3, waiting for transfers between devices, spread_from_first(): lax.ppermute(held, 'ctx', [(b * LAYER, (b + j * stride) * LAYER) for b in...  4.71 us
    ppermute x2, waiting for transfers between devices, spread_from_first(): held = jnp.where(here, lax.ppermute(held, 'ctx', pairs), held)  4.28 us
    ppermute x2, starting transfers between devices, passed_along(): return lax.ppermute(array, 'ctx', pairs)  2.6 us
  transfers between devices with their start and end apart: 16, of which 10 were waited for; matrix products, arithmetic and copies ran while one was open for 4% of the time, Pallas kernels for 0%

profile of v3, /device:TPU:0, one launch (start us, length us, event | category | flops | bytes accessed | tf_op | source)
XLA Modules:
  0.0 85.1 jit_solution(935116749530887911)
XLA Ops:
  0.6 1.8 %exported.1 = (s32[1]{0:T(128)}, s32[1]{0:T(128)}, bf16[2,128,512]{2,1,0:T(8,128)(2,1)S(1)}, bf16[2,128,512]{2,1,0:T(8,128)(2,1)S(1)}) custom-call(s32[32]{0:T(128)} %parents_ref.1, bf16[256,512]{1,0:T(8,128)(2,1)} %k_ref.1, bf16[256,512]{1,0:T(8,128)(2,1)} %v_ref.1), custom_call_target="tpu_custom_call" | custom-call | tf_op jit(solution)/shard_map/exported/pallas_call | solution.py:121
  3.1 82.1 %conditional.1 = (bf16[256,4096]{1,0:T(8,128)(2,1)}, bf16[256,4096]{1,0:T(8,128)(2,1)}, bf16[256,512]{1,0:T(8,128)(2,1)}, bf16[256,512]{1,0:T(8,128)(2,1)}) conditional(s32[]{:T(128)} %bitcast.17, (bf16[2,128,512]{2,1,0:T(8,128)(2,1)S(1)}, bf16[2,128,512]{2,1,0:T(8,128)(2,1)S(1)}, s32[32]{0:T(128)}, bf16[256,4096]{1,0:T(8,128)(2,1)}, ...), branch_computations={%region_0.1_spmd, %region_1.2_spmd} | conditional | flops 6815806 | bytes 39061180 | solution.py:428
  3.1 4.9 %collective-permute-start = (bf16[2,128,512]{2,1,0:T(8,128)(2,1)S(1)}, bf16[2,128,512]{2,1,0:T(8,128)(2,1)S(1)}, u32[]{:S(2)}, u32[]{:S(2)}) collective-permute-start(bf16[2,128,512]{2,1,0:T(8,128)(2,1)S(1)} %get-tuple-element.37), channel_id=1, source_target_pairs={{0,8},{1,9}} | collective-permute-start | bytes 786440 | tf_op jit(solution)/shard_map/cond/branch_0_fun/ppermute | solution.py:43
  8.0 1.7 %collective-permute-start.1 = (bf16[2,128,512]{2,1,0:T(8,128)(2,1)S(1)}, bf16[2,128,512]{2,1,0:T(8,128)(2,1)S(1)}, u32[]{:S(2)}, u32[]{:S(2)}) collective-permute-start(bf16[2,128,512]{2,1,0:T(8,128)(2,1)S(1)} %get-tuple-element.37), channel_id=1, source_target_pairs={{0,16},{1,17}} | collective-permute-start | bytes 786440 | tf_op jit(solution)/shard_map/cond/branch_0_fun/ppermute | solution.py:43
  9.7 1.7 %collective-permute-start.2 = (bf16[2,128,512]{2,1,0:T(8,128)(2,1)S(1)}, bf16[2,128,512]{2,1,0:T(8,128)(2,1)S(1)}, u32[]{:S(2)}, u32[]{:S(2)}) collective-permute-start(bf16[2,128,512]{2,1,0:T(8,128)(2,1)S(1)} %get-tuple-element.37), channel_id=1, source_target_pairs={{0,24},{1,25}} | collective-permute-start | bytes 786440 | tf_op jit(solution)/shard_map/cond/branch_0_fun/ppermute | solution.py:43
  11.4 1.3 %collective-permute-start.3 = (bf16[2,128,512]{2,1,0:T(8,128)(2,1)S(1)}, bf16[2,128,512]{2,1,0:T(8,128)(2,1)S(1)}, u32[]{:S(2)}, u32[]{:S(2)}) collective-permute-start(bf16[2,128,512]{2,1,0:T(8,128)(2,1)S(1)} %get-tuple-element.38), channel_id=1, source_target_pairs={{0,4},{2,6},{4,8},{6,10},{8,12},{10,14},{12,16},{14,18},{16,20},{1... | collective-permute-start | bytes 786440 | tf_op jit(solution)/shard_map/cond/branch_0_fun/ppermute | solution.py:23
  12.8 1.9 %collective-permute-done.1 = bf16[2,128,512]{2,1,0:T(8,128)(2,1)S(1)} collective-permute-done((bf16[2,128,512]{2,1,0:T(8,128)(2,1)S(1)}, bf16[2,128,512]{2,1,0:T(8,128)(2,1)S(1)}, u32[]{:S(2)}, u32[]{:S(2)}) %collective-permute-start.1) | collective-permute-done | bytes 262176 | tf_op jit(solution)/shard_map/cond/branch_0_fun/ppermute | solution.py:43
  14.7 2.8 %collective-permute-done.2 = bf16[2,128,512]{2,1,0:T(8,128)(2,1)S(1)} collective-permute-done((bf16[2,128,512]{2,1,0:T(8,128)(2,1)S(1)}, bf16[2,128,512]{2,1,0:T(8,128)(2,1)S(1)}, u32[]{:S(2)}, u32[]{:S(2)}) %collective-permute-start.2) | collective-permute-done | bytes 262176 | tf_op jit(solution)/shard_map/cond/branch_0_fun/ppermute | solution.py:43
  17.6 3.4 %collective-permute-start.4 = (bf16[2,128,512]{2,1,0:T(8,128)(2,1)S(1)}, bf16[2,128,512]{2,1,0:T(8,128)(2,1)S(1)}, u32[]{:S(2)}, u32[]{:S(2)}) collective-permute-start(bf16[2,128,512]{2,1,0:T(8,128)(2,1)S(1)} %select_select_fusion), channel_id=1, source_target_pairs={{0,4},{8,12},{16,20},{24,28},{1,5},{9,13},{17,21},{25,29}} | collective-permute-start | bytes 786440 | tf_op jit(solution)/shard_map/cond/branch_0_fun/ppermute | solution.py:58
  21.0 0.7 collective-permute-start.5
  21.7 3.2 %collective-permute-done.4 = bf16[2,128,512]{2,1,0:T(8,128)(2,1)S(1)} collective-permute-done((bf16[2,128,512]{2,1,0:T(8,128)(2,1)S(1)}, bf16[2,128,512]{2,1,0:T(8,128)(2,1)S(1)}, u32[]{:S(2)}, u32[]{:S(2)}) %collective-permute-start.4) | collective-permute-done | bytes 262176 | tf_op jit(solution)/shard_map/cond/branch_0_fun/ppermute | solution.py:58
  24.9 2.0 %collective-permute-start.7 = (bf16[2,256,512]{2,1,0:T(8,128)(2,1)S(1)}, bf16[2,256,512]{2,1,0:T(8,128)(2,1)S(1)}, u32[]{:S(2)}, u32[]{:S(2)}) collective-permute-start(bf16[2,256,512]{2,1,0:T(8,128)(2,1)S(1)} %pad_maximum_fusion), channel_id=1, source_target_pairs={{0,2},{2,0},{4,6},{6,4},{8,10},{10,8},{12,14},{14,12},{16,18},{18,... | collective-permute-start | bytes 1572872 | tf_op jit(solution)/shard_map/cond/branch_0_fun/ppermute | solution.py:395
  27.0 1.9 %collective-permute-start.6 = (bf16[2,128,512]{2,1,0:T(8,128)(2,1)S(1)}, bf16[2,128,512]{2,1,0:T(8,128)(2,1)S(1)}, u32[]{:S(2)}, u32[]{:S(2)}) collective-permute-start(bf16[2,128,512]{2,1,0:T(8,128)(2,1)S(1)} %broadcast_select_fusion), channel_id=1, source_target_pairs={{0,2},{4,6},{8,10},{12,14},{16,18},{20,22},{24,26},{28,30},{1,3},{... | collective-permute-start | bytes 786440 | tf_op jit(solution)/shard_map/cond/branch_0_fun/ppermute | solution.py:58
  28.9 1.1 %collective-permute-done.6 = bf16[2,128,512]{2,1,0:T(8,128)(2,1)S(1)} collective-permute-done((bf16[2,128,512]{2,1,0:T(8,128)(2,1)S(1)}, bf16[2,128,512]{2,1,0:T(8,128)(2,1)S(1)}, u32[]{:S(2)}, u32[]{:S(2)}) %collective-permute-start.6) | collective-permute-done | bytes 262176 | tf_op jit(solution)/shard_map/cond/branch_0_fun/ppermute | solution.py:58
  30.1 21.3 %tree_attention_6.1 = (bf16[256,4096]{1,0:T(8,128)(2,1)}, bf16[256,4096]{1,0:T(8,128)(2,1)}, f32[2,256,512]{2,1,0:T(8,128)S(1)}, f32[2,128,512]{2,1,0:T(8,128)S(...) custom-call(s32[32]{0:T(128)S(1)} %copy-done.3, ...), custom_call_target="tpu_custom_call" | custom-call | tf_op jit(solution)/shard_map/cond/branch_0_fun/tree_attention_6/pallas_call | solution.py:330
  51.4 1.3 %collective-permute-start.8 = (bf16[2,128,512]{2,1,0:T(8,128)(2,1)S(1)}, bf16[2,128,512]{2,1,0:T(8,128)(2,1)S(1)}, u32[]{:S(2)}, u32[]{:S(2)}) collective-permute-start(bf16[2,128,512]{2,1,0:T(8,128)(2,1)S(1)} %convert_element_type.89), channel_id=1, source_target_pairs={{2,0},{6,4},{10,8},{14,12},{18,16},{22,20},{26,24},{30,28},{3,1},{... | collective-permute-start | bytes 786440 | tf_op jit(solution)/shard_map/cond/branch_0_fun/ppermute | solution.py:75
  52.7 1.2 %collective-permute-start.10 = (bf16[2,256,512]{2,1,0:T(8,128)(2,1)S(1)}, bf16[2,256,512]{2,1,0:T(8,128)(2,1)}, u32[]{:S(2)}, u32[]{:S(2)}) collective-permute-start(bf16[2,256,512]{2,1,0:T(8,128)(2,1)S(1)} %get-tuple-element.50), channel_id=1, source_target_pairs={{0,2},{2,0},{4,6},{6,4},{8,10},{10,8},{12,14},{14,12},{16,18},{18,... | collective-permute-start | bytes 1572872 | tf_op jit(solution)/shard_map/cond/branch_0_fun/ppermute | solution.py:406
  53.9 0.9 %collective-permute-done.8 = bf16[2,128,512]{2,1,0:T(8,128)(2,1)S(1)} collective-permute-done((bf16[2,128,512]{2,1,0:T(8,128)(2,1)S(1)}, bf16[2,128,512]{2,1,0:T(8,128)(2,1)S(1)}, u32[]{:S(2)}, u32[]{:S(2)}) %collective-permute-start.8) | collective-permute-done | bytes 262176 | tf_op jit(solution)/shard_map/cond/branch_0_fun/ppermute | solution.py:75
  54.9 1.3 %collective-permute-start.9 = (bf16[2,128,512]{2,1,0:T(8,128)(2,1)S(1)}, bf16[2,128,512]{2,1,0:T(8,128)(2,1)S(1)}, u32[]{:S(2)}, u32[]{:S(2)}) collective-permute-start(bf16[2,128,512]{2,1,0:T(8,128)(2,1)S(1)} %fusion.6), channel_id=1, source_target_pairs={{4,0},{8,12},{16,20},{24,28},{5,1},{9,13},{17,21},{25,29}} | collective-permute-start | bytes 786440 | tf_op jit(solution)/shard_map/cond/branch_0_fun/ppermute | solution.py:75
  56.9 6.3 %collective-permute-done.9 = bf16[2,128,512]{2,1,0:T(8,128)(2,1)S(1)} collective-permute-done((bf16[2,128,512]{2,1,0:T(8,128)(2,1)S(1)}, bf16[2,128,512]{2,1,0:T(8,128)(2,1)S(1)}, u32[]{:S(2)}, u32[]{:S(2)}) %collective-permute-start.9) | collective-permute-done | bytes 262176 | tf_op jit(solution)/shard_map/cond/branch_0_fun/ppermute | solution.py:75
  63.3 1.3 %collective-permute-start.15 = (bf16[2,128,512]{2,1,0:T(8,128)(2,1)S(1)}, bf16[2,128,512]{2,1,0:T(8,128)(2,1)S(1)}, u32[]{:S(2)}, u32[]{:S(2)}) collective-permute-start(bf16[2,128,512]{2,1,0:T(8,128)(2,1)S(1)} %fusion.7), channel_id=1, source_target_pairs={{28,0},{29,1}} | collective-permute-start | bytes 786440 | tf_op jit(solution)/shard_map/cond/branch_0_fun/ppermute | solution.py:75
  64.6 1.3 %collective-permute-start.14 = (bf16[2,128,512]{2,1,0:T(8,128)(2,1)S(1)}, bf16[2,128,512]{2,1,0:T(8,128)(2,1)S(1)}, u32[]{:S(2)}, u32[]{:S(2)}) collective-permute-start(bf16[2,128,512]{2,1,0:T(8,128)(2,1)S(1)} %fusion.7), channel_id=1, source_target_pairs={{20,0},{21,1}} | collective-permute-start | bytes 786440 | tf_op jit(solution)/shard_map/cond/branch_0_fun/ppermute | solution.py:75
  65.9 1.3 %collective-permute-start.13 = (bf16[2,128,512]{2,1,0:T(8,128)(2,1)S(1)}, bf16[2,128,512]{2,1,0:T(8,128)(2,1)}, u32[]{:S(2)}, u32[]{:S(2)}) collective-permute-start(bf16[2,128,512]{2,1,0:T(8,128)(2,1)S(1)} %fusion.7), channel_id=1, source_target_pairs={{12,0},{13,1}} | collective-permute-start | bytes 786440 | tf_op jit(solution)/shard_map/cond/branch_0_fun/ppermute | solution.py:75
  68.0 1.0 %add_convert_fusion = bf16[2,128,512]{2,1,0:T(8,128)(2,1)S(1)} fusion(bf16[2,128,512]{2,1,0:T(8,128)(2,1)S(1)} %get-tuple-element.48, bf16[2,256,512]{2,1,0:T(8,128)(2,1)} %collective-permute-done.10), kind=kLoop, calls=%fused_computation.13 | loop fusion | flops 524288 | bytes 786432 | tf_op jit(solution)/shard_map/cond/branch_0_fun/convert_element_type | solution.py:410
  69.0 1.3 %collective-permute-start.11 = (bf16[2,128,512]{2,1,0:T(8,128)(2,1)S(1)}, bf16[2,128,512]{2,1,0:T(8,128)(2,1)S(1)}, u32[]{:S(2)}, u32[]{:S(2)}) collective-permute-start(bf16[2,128,512]{2,1,0:T(8,128)(2,1)S(1)} %add_convert_fusion), channel_id=1, source_target_pairs={{4,0},{6,2},{8,4},{10,6},{12,8},{14,10},{16,12},{18,14},{20,16},{2... | collective-permute-start | bytes 786440 | tf_op jit(solution)/shard_map/cond/branch_0_fun/ppermute | solution.py:23
  70.3 4.5 %collective-permute-done.15 = bf16[2,128,512]{2,1,0:T(8,128)(2,1)S(1)} collective-permute-done((bf16[2,128,512]{2,1,0:T(8,128)(2,1)S(1)}, bf16[2,128,512]{2,1,0:T(8,128)(2,1)S(1)}, u32[]{:S(2)}, u32[]{:S(2)}) %collective-permute-start.15) | collective-permute-done | bytes 262176 | tf_op jit(solution)/shard_map/cond/branch_0_fun/ppermute | solution.py:75
  74.8 2.8 %collective-permute-done.14 = bf16[2,128,512]{2,1,0:T(8,128)(2,1)S(1)} collective-permute-done((bf16[2,128,512]{2,1,0:T(8,128)(2,1)S(1)}, bf16[2,128,512]{2,1,0:T(8,128)(2,1)S(1)}, u32[]{:S(2)}, u32[]{:S(2)}) %collective-permute-start.14) | collective-permute-done | bytes 262176 | tf_op jit(solution)/shard_map/cond/branch_0_fun/ppermute | solution.py:75
  77.6 2.8 %collective-permute-done.13 = bf16[2,128,512]{2,1,0:T(8,128)(2,1)} collective-permute-done((bf16[2,128,512]{2,1,0:T(8,128)(2,1)S(1)}, bf16[2,128,512]{2,1,0:T(8,128)(2,1)}, u32[]{:S(2)}, u32[]{:S(2)}) %collective-permute-start.13) | collective-permute-done | bytes 262176 | tf_op jit(solution)/shard_map/cond/branch_0_fun/ppermute | solution.py:75
  80.4 1.1 %convert_add_fusion = f32[2,128,512]{2,1,0:T(8,128)S(1)} fusion(bf16[2,128,512]{2,1,0:T(8,128)(2,1)S(1)} %collective-permute-done.15, bf16[2,128,512]{2,1,0:T(8,128)(2,1)S(1)} %collective-permute-done.14, bf16[2,128,512]{2,1,0:T(8,128)(2,1)} %collective-permute-done.13, bf16[2,128,512]{2,1,0:T(8,128)(2,1)S(1)} %collective-permute-done.9, ...), kind=kLoop, calls=%fused_computation.11 | loop fusion | flops 1310720 | bytes 2359296 | tf_op jit(solution)/shard_map/cond/branch_0_fun/add | solution.py:79
  81.6 1.4 %collective-permute-done.11 = bf16[2,128,512]{2,1,0:T(8,128)(2,1)S(1)} collective-permute-done((bf16[2,128,512]{2,1,0:T(8,128)(2,1)S(1)}, bf16[2,128,512]{2,1,0:T(8,128)(2,1)S(1)}, u32[]{:S(2)}, u32[]{:S(2)}) %collective-permute-start.11) | collective-permute-done | bytes 262176 | tf_op jit(solution)/shard_map/cond/branch_0_fun/ppermute | solution.py:23
  83.0 1.1 %add_bitcast_fusion = (f32[128,512]{1,0:T(8,128)S(1)}, f32[128,512]{1,0:T(8,128)S(1)}) fusion(bf16[2,128,512]{2,1,0:T(8,128)(2,1)S(1)} %collective-permute-done.12, bf16[2,128,512]{2,1,0:T(8,128)(2,1)S(1)} %collective-permute-done.11, bf16[2,256,512]{2,1,0:T(8,128)(2,1)} %collective-permute-done.10, pred[]{:T(512)S(6)} %eq.77), kind=kLoop, calls=%fused_computation.18 | loop fusion | flops 786432 | bytes 1310721 | tf_op jit(solution)/shard_map/cond/branch_0_fun/mul | solution.py:420
  84.1 1.1 %fusion.1 = (bf16[256,512]{1,0:T(8,128)(2,1)}, bf16[256,512]{1,0:T(8,128)(2,1)}) fusion(f32[2,256,512]{2,1,0:T(8,128)S(1)} %get-tuple-element.46, f32[128,512]{1,0:T(8,128)S(1)} %get-tuple-element.89, f32[128,512]{1,0:T(8,128)S(1)} %get-tuple-element.87, f32[256]{0:T(256)S(1)} %get-tuple-element.91, f32[256]{0:T(256)S(1)} %get-tuple-element.92, ...), kind=kLoop, calls=%fused_computation.3 | loop fusion | flops 1310720 | bytes 2623488 | tf_op jit(solution)/shard_map/cond/branch_0_fun/convert_element_type | solution.py:421
  (24 shorter events, 1.8 us)
Async XLA Ops:
  3.1 27.0 %copy-start.3 = (s32[32]{0:T(128)S(1)}, s32[32]{0:T(128)}, u32[]{:S(2)}) copy-start(s32[32]{0:T(128)} %get-tuple-element.28.parents_ref) | copy-start | bytes 388 | tf_op jit(solution)/shard_map/cond
  3.1 9.7 %collective-permute-start = (bf16[2,128,512]{2,1,0:T(8,128)(2,1)S(1)}, bf16[2,128,512]{2,1,0:T(8,128)(2,1)S(1)}, u32[]{:S(2)}, u32[]{:S(2)}) collective-permute-start(bf16[2,128,512]{2,1,0:T(8,128)(2,1)S(1)} %get-tuple-element.37), channel_id=1, source_target_pairs={{0,8},{1,9}} | collective-permute-start | bytes 786440 | tf_op jit(solution)/shard_map/cond/branch_0_fun/ppermute | solution.py:43
  8.0 6.7 %collective-permute-start.1 = (bf16[2,128,512]{2,1,0:T(8,128)(2,1)S(1)}, bf16[2,128,512]{2,1,0:T(8,128)(2,1)S(1)}, u32[]{:S(2)}, u32[]{:S(2)}) collective-permute-start(bf16[2,128,512]{2,1,0:T(8,128)(2,1)S(1)} %get-tuple-element.37), channel_id=1, source_target_pairs={{0,16},{1,17}} | collective-permute-start | bytes 786440 | tf_op jit(solution)/shard_map/cond/branch_0_fun/ppermute | solution.py:43
  9.7 7.8 %collective-permute-start.2 = (bf16[2,128,512]{2,1,0:T(8,128)(2,1)S(1)}, bf16[2,128,512]{2,1,0:T(8,128)(2,1)S(1)}, u32[]{:S(2)}, u32[]{:S(2)}) collective-permute-start(bf16[2,128,512]{2,1,0:T(8,128)(2,1)S(1)} %get-tuple-element.37), channel_id=1, source_target_pairs={{0,24},{1,25}} | collective-permute-start | bytes 786440 | tf_op jit(solution)/shard_map/cond/branch_0_fun/ppermute | solution.py:43
  11.4 6.1 %collective-permute-start.3 = (bf16[2,128,512]{2,1,0:T(8,128)(2,1)S(1)}, bf16[2,128,512]{2,1,0:T(8,128)(2,1)S(1)}, u32[]{:S(2)}, u32[]{:S(2)}) collective-permute-start(bf16[2,128,512]{2,1,0:T(8,128)(2,1)S(1)} %get-tuple-element.38), channel_id=1, source_target_pairs={{0,4},{2,6},{4,8},{6,10},{8,12},{10,14},{12,16},{14,18},{16,20},{1... | collective-permute-start | bytes 786440 | tf_op jit(solution)/shard_map/cond/branch_0_fun/ppermute | solution.py:23
  17.6 7.3 %collective-permute-start.4 = (bf16[2,128,512]{2,1,0:T(8,128)(2,1)S(1)}, bf16[2,128,512]{2,1,0:T(8,128)(2,1)S(1)}, u32[]{:S(2)}, u32[]{:S(2)}) collective-permute-start(bf16[2,128,512]{2,1,0:T(8,128)(2,1)S(1)} %select_select_fusion), channel_id=1, source_target_pairs={{0,4},{8,12},{16,20},{24,28},{1,5},{9,13},{17,21},{25,29}} | collective-permute-start | bytes 786440 | tf_op jit(solution)/shard_map/cond/branch_0_fun/ppermute | solution.py:58
  21.0 3.9 %collective-permute-start.5 = (bf16[2,128,512]{2,1,0:T(8,128)(2,1)S(1)}, bf16[2,128,512]{2,1,0:T(8,128)(2,1)S(1)}, u32[]{:S(2)}, u32[]{:S(2)}) collective-permute-start(bf16[2,128,512]{2,1,0:T(8,128)(2,1)S(1)} %get-tuple-element.38), channel_id=1, source_target_pairs={{2,8},{6,12},{10,16},{14,20},{18,24},{22,28},{3,9},{7,13},{11,17},... | collective-permute-start | bytes 786440 | tf_op jit(solution)/shard_map/cond/branch_0_fun/ppermute | solution.py:393
  24.9 5.1 %collective-permute-start.7 = (bf16[2,256,512]{2,1,0:T(8,128)(2,1)S(1)}, bf16[2,256,512]{2,1,0:T(8,128)(2,1)S(1)}, u32[]{:S(2)}, u32[]{:S(2)}) collective-permute-start(bf16[2,256,512]{2,1,0:T(8,128)(2,1)S(1)} %pad_maximum_fusion), channel_id=1, source_target_pairs={{0,2},{2,0},{4,6},{6,4},{8,10},{10,8},{12,14},{14,12},{16,18},{18,... | collective-permute-start | bytes 1572872 | tf_op jit(solution)/shard_map/cond/branch_0_fun/ppermute | solution.py:395
  27.0 3.1 %collective-permute-start.6 = (bf16[2,128,512]{2,1,0:T(8,128)(2,1)S(1)}, bf16[2,128,512]{2,1,0:T(8,128)(2,1)S(1)}, u32[]{:S(2)}, u32[]{:S(2)}) collective-permute-start(bf16[2,128,512]{2,1,0:T(8,128)(2,1)S(1)} %broadcast_select_fusion), channel_id=1, source_target_pairs={{0,2},{4,6},{8,10},{12,14},{16,18},{20,22},{24,26},{28,30},{1,3},{... | collective-permute-start | bytes 786440 | tf_op jit(solution)/shard_map/cond/branch_0_fun/ppermute | solution.py:58
  51.4 2.5 %copy-start = (bf16[2,128,512]{2,1,0:T(8,128)(2,1)}, bf16[2,128,512]{2,1,0:T(8,128)(2,1)S(1)}, u32[]{:S(2)}) copy-start(bf16[2,128,512]{2,1,0:T(8,128)(2,1)S(1)} %get-tuple-element.52) | copy-start | bytes 786436 | tf_op jit(solution)/shard_map/cond
  51.4 3.4 %collective-permute-start.8 = (bf16[2,128,512]{2,1,0:T(8,128)(2,1)S(1)}, bf16[2,128,512]{2,1,0:T(8,128)(2,1)S(1)}, u32[]{:S(2)}, u32[]{:S(2)}) collective-permute-start(bf16[2,128,512]{2,1,0:T(8,128)(2,1)S(1)} %convert_element_type.89), channel_id=1, source_target_pairs={{2,0},{6,4},{10,8},{14,12},{18,16},{22,20},{26,24},{30,28},{3,1},{... | collective-permute-start | bytes 786440 | tf_op jit(solution)/shard_map/cond/branch_0_fun/ppermute | solution.py:75
  52.7 4.2 %collective-permute-start.10 = (bf16[2,256,512]{2,1,0:T(8,128)(2,1)S(1)}, bf16[2,256,512]{2,1,0:T(8,128)(2,1)}, u32[]{:S(2)}, u32[]{:S(2)}) collective-permute-start(bf16[2,256,512]{2,1,0:T(8,128)(2,1)S(1)} %get-tuple-element.50), channel_id=1, source_target_pairs={{0,2},{2,0},{4,6},{6,4},{8,10},{10,8},{12,14},{14,12},{16,18},{18,... | collective-permute-start | bytes 1572872 | tf_op jit(solution)/shard_map/cond/branch_0_fun/ppermute | solution.py:406
  54.9 12.4 %copy-start.1 = (bf16[2,128,512]{2,1,0:T(8,128)(2,1)S(1)}, bf16[2,128,512]{2,1,0:T(8,128)(2,1)}, u32[]{:S(2)}) copy-start(bf16[2,128,512]{2,1,0:T(8,128)(2,1)} %copy-done) | copy-start | bytes 786436 | tf_op jit(solution)/shard_map/cond
  54.9 8.3 %collective-permute-start.9 = (bf16[2,128,512]{2,1,0:T(8,128)(2,1)S(1)}, bf16[2,128,512]{2,1,0:T(8,128)(2,1)S(1)}, u32[]{:S(2)}, u32[]{:S(2)}) collective-permute-start(bf16[2,128,512]{2,1,0:T(8,128)(2,1)S(1)} %fusion.6), channel_id=1, source_target_pairs={{4,0},{8,12},{16,20},{24,28},{5,1},{9,13},{17,21},{25,29}} | collective-permute-start | bytes 786440 | tf_op jit(solution)/shard_map/cond/branch_0_fun/ppermute | solution.py:75
  63.3 11.5 %collective-permute-start.15 = (bf16[2,128,512]{2,1,0:T(8,128)(2,1)S(1)}, bf16[2,128,512]{2,1,0:T(8,128)(2,1)S(1)}, u32[]{:S(2)}, u32[]{:S(2)}) collective-permute-start(bf16[2,128,512]{2,1,0:T(8,128)(2,1)S(1)} %fusion.7), channel_id=1, source_target_pairs={{28,0},{29,1}} | collective-permute-start | bytes 786440 | tf_op jit(solution)/shard_map/cond/branch_0_fun/ppermute | solution.py:75
  64.6 12.9 %collective-permute-start.14 = (bf16[2,128,512]{2,1,0:T(8,128)(2,1)S(1)}, bf16[2,128,512]{2,1,0:T(8,128)(2,1)S(1)}, u32[]{:S(2)}, u32[]{:S(2)}) collective-permute-start(bf16[2,128,512]{2,1,0:T(8,128)(2,1)S(1)} %fusion.7), channel_id=1, source_target_pairs={{20,0},{21,1}} | collective-permute-start | bytes 786440 | tf_op jit(solution)/shard_map/cond/branch_0_fun/ppermute | solution.py:75
  65.9 14.5 %collective-permute-start.13 = (bf16[2,128,512]{2,1,0:T(8,128)(2,1)S(1)}, bf16[2,128,512]{2,1,0:T(8,128)(2,1)}, u32[]{:S(2)}, u32[]{:S(2)}) collective-permute-start(bf16[2,128,512]{2,1,0:T(8,128)(2,1)S(1)} %fusion.7), channel_id=1, source_target_pairs={{12,0},{13,1}} | collective-permute-start | bytes 786440 | tf_op jit(solution)/shard_map/cond/branch_0_fun/ppermute | solution.py:75
  67.3 14.3 %collective-permute-start.12 = (bf16[2,128,512]{2,1,0:T(8,128)(2,1)S(1)}, bf16[2,128,512]{2,1,0:T(8,128)(2,1)S(1)}, u32[]{:S(2)}, u32[]{:S(2)}) collective-permute-start(bf16[2,128,512]{2,1,0:T(8,128)(2,1)S(1)} %copy-done.1), channel_id=1, source_target_pairs={{8,2},{12,6},{16,10},{20,14},{24,18},{28,22},{9,3},{13,7},{17,11},... | collective-permute-start | bytes 786440 | tf_op jit(solution)/shard_map/cond/branch_0_fun/ppermute | solution.py:407
  69.0 14.0 %collective-permute-start.11 = (bf16[2,128,512]{2,1,0:T(8,128)(2,1)S(1)}, bf16[2,128,512]{2,1,0:T(8,128)(2,1)S(1)}, u32[]{:S(2)}, u32[]{:S(2)}) collective-permute-start(bf16[2,128,512]{2,1,0:T(8,128)(2,1)S(1)} %add_convert_fusion), channel_id=1, source_target_pairs={{4,0},{6,2},{8,4},{10,6},{12,8},{14,10},{16,12},{18,14},{20,16},{2... | collective-permute-start | bytes 786440 | tf_op jit(solution)/shard_map/cond/branch_0_fun/ppermute | solution.py:23
